TPU v7x, 32 devices: a whole 2x2x4 slice. The times are simulated.
32 devices in a mesh: dp: 4 (over z), seq: 8 (over y, x, core).
Axes of the slice: x: 2, y: 2, z: 4, core: 2. Of those that a mesh axis runs over, the one named last changes fastest.
Arguments:
- saved_codes: bfloat16 [4, 1024, 1536], P('dp', 'seq'), may hold values from -6 to 6
- code_scales: float32 [4, 12, 1024], P('dp', None, 'seq'), may hold values from 0.25 to 4
- lengths: int32 [4], replicated, may hold values from 128 to 1024, as said below
- in_weight: bfloat16 [3072, 1536], P('dp'), may hold values from -0.15625 to 0.15625
- conv_kernel: float32 [31, 1536], replicated, may hold values from -1 to 1
- bn_gain: float32 [1536], replicated, may hold values from 0.1 to 1.9
- bn_shift: float32 [1536], replicated, may hold values from -3 to 3
- out_grad: bfloat16 [4, 1024, 1536], P('dp', 'seq'), may hold values from -6 to 6
Outputs:
- in_grad: bfloat16 [4, 1024, 1536], P('dp', 'seq')
- weight_grad: float32 [3072, 1536], P('dp')
- kernel_grad: float32 [31, 1536], replicated
- gain_grad: float32 [1536], replicated
- shift_grad: float32 [1536], replicated
Inputs may be any that keep to these rules, and one draw needn't show every extreme that they name: `lengths`: at least one recording has exactly 1024 valid frames.
All inputs are finite; a program needn't handle non-finite values.
Results may differ from a plain program's by a relative error of at most 0.0067.
Values may be sent and summed in bfloat16 or wider, within the bound.
A program may use at most 128 MiB of HBM per device.

v0:
```python
import jax
import jax.numpy as jnp
from jax import lax
from jax.sharding import PartitionSpec as P

EPS = 1e-05


def padded_2(cells, sides, width):
    for axis, dim in sides:
        count = lax.axis_size(axis)
        ends = count - 1
        head = lax.slice_in_dim(cells, 0, width, axis=dim)
        tail = lax.slice_in_dim(cells, cells.shape[dim] - width, cells.shape[dim], axis=dim)
        cells = jnp.concatenate(
            [
                lax.ppermute(tail, axis, [(i, (i + 1) % count) for i in range(ends)]),
                cells,
                lax.ppermute(head, axis, [((i + 1) % count, i) for i in range(ends)]),
            ],
            axis=dim,
        )
    return cells


def restore(quantized, scales):
    per_channel = jnp.repeat(scales.T, 128, axis=1)
    return (quantized.astype(jnp.float32) * per_channel).astype(jnp.bfloat16)


def depthwise(padded, kernel, frames):
    running = jnp.zeros((frames, padded.shape[1]), jnp.float32)
    for offset in range(kernel.shape[0]):
        running = running + kernel[offset] * padded[offset : offset + frames].astype(jnp.float32)
    return running


def per_device(
    saved_codes, code_scales, lengths, in_weight, conv_kernel, bn_gain, bn_shift, out_grad
):
    frames = saved_codes.shape[1]
    feature_width = saved_codes.shape[2]
    tap_count = conv_kernel.shape[0]
    half_span = (tap_count - 1) // 2
    groups = lengths.shape[0]
    group_at = lax.axis_index("dp")
    length = jnp.sum(jnp.where(jnp.arange(groups, dtype=jnp.int32) == group_at, lengths, 0))
    counted = jnp.sum(lengths).astype(jnp.float32)
    first_frame = lax.axis_index("seq") * frames
    valid_mask = (first_frame + jnp.arange(frames, dtype=jnp.int32) < length).astype(jnp.float32)[
        :, None
    ]
    restored = restore(saved_codes[0], code_scales[0])
    weights = lax.all_gather(in_weight, "dp", axis=0, tiled=True)
    pre_act = lax.dot_general(
        restored, weights, (((1,), (1,)), ((), ())), preferred_element_type=jnp.float32
    )
    linear = pre_act[:, :feature_width]
    gate_part = jax.nn.sigmoid(pre_act[:, feature_width:])
    gated = (linear * gate_part * valid_mask).astype(jnp.bfloat16)
    gated_pad = padded_2(gated, (("seq", 0),), half_span)
    conv_out = depthwise(gated_pad, conv_kernel, frames)
    mean_value = lax.psum(jnp.sum(conv_out * valid_mask, axis=0), ("dp", "seq")) / counted
    centered = (conv_out - mean_value) * valid_mask
    variance = lax.psum(jnp.sum(centered * centered, axis=0), ("dp", "seq")) / counted
    inverse = lax.rsqrt(variance + EPS)
    normed = (conv_out - mean_value) * inverse
    shaped = bn_gain * normed + bn_shift
    smooth = jax.nn.sigmoid(shaped)
    grad_shaped = (
        out_grad[0].astype(jnp.float32) * valid_mask * smooth * (1.0 + shaped * (1.0 - smooth))
    )
    shift_grad, gain_grad = lax.psum(
        (jnp.sum(grad_shaped, axis=0), jnp.sum(grad_shaped * normed, axis=0)), ("dp", "seq")
    )
    grad_conv = (
        bn_gain * inverse * (grad_shaped - (shift_grad + normed * gain_grad) / counted) * valid_mask
    )
    kernel_part = jnp.stack(
        [
            jnp.sum(grad_conv * gated_pad[offset : offset + frames].astype(jnp.float32), axis=0)
            for offset in range(tap_count)
        ]
    )
    kernel_grad = lax.psum(kernel_part, ("dp", "seq"))
    grad_pad = padded_2(grad_conv, (("seq", 0),), half_span)
    grad_gated = depthwise(grad_pad, conv_kernel[::-1], frames) * valid_mask
    grad_pre = jnp.concatenate(
        [grad_gated * gate_part, grad_gated * linear * gate_part * (1.0 - gate_part)], axis=1
    ).astype(jnp.bfloat16)
    in_grad = jnp.dot(grad_pre, weights, preferred_element_type=jnp.float32)
    own_columns = lax.all_to_all(grad_pre[None], "dp", split_axis=2, concat_axis=0, tiled=True)
    local_rows = lax.dot_general(
        own_columns,
        lax.all_gather(restored[None], "dp", axis=0, tiled=True),
        (((0, 1), (0, 1)), ((), ())),
        preferred_element_type=jnp.float32,
    )
    weight_grad = lax.psum(local_rows, "seq")
    return (in_grad.astype(jnp.bfloat16)[None], weight_grad, kernel_grad, gain_grad, shift_grad)


def solution(mesh):
    in_specs = (
        P("dp", "seq", None),
        P("dp", None, "seq"),
        P(),
        P("dp", None),
        P(),
        P(),
        P(),
        P("dp", "seq", None),
    )
    out_specs = (P("dp", "seq", None), P("dp", None), P(), P(), P())
    return jax.shard_map(
        per_device, mesh=mesh, in_specs=in_specs, out_specs=out_specs, check_vma=False
    )
```

profile of v0, /device:TPU:0, one launch (start us, length us, event | category | flops | bytes accessed | tf_op | source)
XLA Modules:
  0.0 607.7 jit_solution(5439914261031607796)
XLA Ops:
  7.2 0.0 all-gather.3.cloned.1.call-start
  7.3 0.7 all-gather.3.cloned.1.call-update
  7.9 0.0 all-gather.5.cloned.1.call-start
  8.0 0.2 copy-done.10
  8.2 0.2 copy.21
  8.4 0.0 copy-start
  8.4 0.1 fusion.150
  8.5 0.6 fusion.193
  9.2 0.6 compare_convert_fusion
  9.8 0.9 slice_reduce_fusion.30
  10.8 168.2 %all-gather.3.cloned.1.call-done = bf16[3072,1536]{1,0:T(8,128)(2,1)} async-done(((bf16[768,1536]{1,0:T(8,128)(2,1)}), bf16[3072,1536]{1,0:T(8,128)(2,1)}) %all-gather.3.cloned.1.call-update) | async-done | bytes 9437200 | tf_op jit(solution)/shard_map/all_gather | solution.py:54
  179.1 6.9 %fusion.199 = f32[128,3072]{1,0:T(8,128)S(1)} fusion(bf16[128,1536]{0,1:T(8,128)(2,1)S(1)} %fusion.150, bf16[3072,1536]{1,0:T(8,128)(2,1)} %all-gather.3.cloned.1.call-done), kind=kOutput, calls=%fused_computation.398 | convolution fusion | flops 1207959552 | bytes 11403264 | tf_op jit(solution)/shard_map/dot_general | solution.py:55
  186.0 0.2 multiply_convert_fusion.2
  186.2 0.0 copy-start.1
  186.2 1.4 collective-permute-start.1
  187.7 3.0 collective-permute-start
  190.7 0.8 slice_reduce_fusion.29
  192.2 0.0 collective-permute-done.1
  192.2 0.0 copy-start.8
  192.3 5.1 multiply_reduce_fusion.2
  197.4 40.2 %psum.42 = f32[1536]{0:T(1024)S(1)} all-reduce(f32[1536]{0:T(1024)S(1)} %get-tuple-element.78), channel_id=1, replica_groups=mesh['dp'=4,'seq'=8] {'dp','seq'}, use_global_device_ids=true, to_apply=%region_2.3 | all-reduce | flops 1536 | bytes 12288 | tf_op jit(solution)/shard_map/psum | solution.py:63
  237.6 0.2 multiply_reduce_fusion.1
  237.8 42.5 %psum.43 = f32[1536]{0:T(1024)S(1)} all-reduce(f32[1536]{0:T(1024)S(1)} %multiply_reduce_fusion.1), channel_id=1, replica_groups=mesh['dp'=4,'seq'=8] {'dp','seq'}, use_global_device_ids=true, to_apply=%region_5.6 | all-reduce | flops 1536 | bytes 12288 | tf_op jit(solution)/shard_map/psum | solution.py:65
  280.3 1.3 fusion.195
  281.6 1.2 fusion.192
  282.9 38.3 %all-reduce = (f32[1536]{0:T(1024)}, f32[1536]{0:T(1024)}) all-reduce(f32[1536]{0:T(1024)S(1)} %get-tuple-element.36, f32[1536]{0:T(1024)S(1)} %get-tuple-element.35), channel_id=1, replica_groups=mesh['dp'=4,'seq'=8] {'dp','seq'}, use_global_device_ids=true, to_apply=%region_9.10 | all-reduce | flops 3072 | bytes 24576 | tf_op jit(solution)/shard_map/psum | solution.py:73
  321.1 3.8 fusion.148
  324.9 1.3 collective-permute-start.3
  326.2 3.2 collective-permute-start.2
  329.5 1.1 fusion.151
  330.5 0.9 copy.23
  331.5 0.0 all-gather.5.cloned.1.call-update
  331.5 5.4 multiply_convert_fusion.1
  336.9 0.3 multiply_convert_fusion
  337.2 0.0 copy-start.4
  337.2 0.4 copy-done.2
  337.6 0.3 copy-done.4
  337.9 0.1 pad_maximum_fusion.2
  338.0 1.9 copy.22
  339.9 0.5 broadcast.68
  340.5 17.0 %reduce.62 = bf16[3072,128]{1,0:T(8,128)(2,1)S(1)} reduce(bf16[3072,1,128]{2,1,0:T(2,128)(2,1)S(1)} %bitcast.43, bf16[]{:T(256)} %broadcast.68), dimensions={1}, to_apply=%bitcast.34.reduce_sub_computation | reduce | bytes 1572866
  357.4 1.0 reshape.100
  358.4 3.5 all-to-all-start
  361.9 0.0 copy-start.9
  361.9 0.0 all-reduce.6.cloned.1.call-start
  362.0 0.7 fusion.118
  362.9 1.1 fusion.127
  364.2 0.8 fusion.147
  365.3 2.8 stack.127
  368.0 0.0 all-reduce.6.cloned.1.call-update
  368.1 0.3 all-reduce.4.cloned.1.call-start
  368.3 18.3 %all-to-all-done = bf16[4,2,49152]{2,1,0:T(2,128)(2,1)S(1)} async-done(((bf16[4,2,49152]{2,1,0:T(2,128)(2,1)}), bf16[4,2,49152]{2,1,0:T(2,128)(2,1)S(1)}, u32[]{:S(2)}, u32[]{:S(2)}) %all-to-all-start) | async-done | bytes 786464 | tf_op jit(solution)/shard_map/all_to_all | solution.py:92
  386.6 0.7 reshape.101
  387.4 0.1 copy.25
  387.5 0.0 all-gather.5.cloned.1.call-done
  387.5 4.4 convolution_bitcast_fusion
  391.9 0.0 all-reduce.4.cloned.1.call-update
  391.9 1.0 copy-done.3
  392.9 0.1 copy-done.5
  393.0 5.8 fusion
  398.9 105.5 %all-reduce.6.cloned.1.call-done = f32[31,1536]{1,0:T(8,128)} async-done(((f32[31,1536]{1,0:T(8,128)}), f32[31,1536]{1,0:T(8,128)}) %all-reduce.6.cloned.1.call-update) | async-done | bytes 190480 | tf_op jit(solution)/shard_map/psum | solution.py:85
  504.4 91.3 %all-reduce.4.cloned.1.call-done = f32[768,1536]{1,0:T(8,128)} async-done(((f32[768,1536]{1,0:T(8,128)}), f32[768,1536]{1,0:T(8,128)}) %all-reduce.4.cloned.1.call-update) | async-done | bytes 4718608 | tf_op jit(solution)/shard_map/psum | solution.py:99
  595.7 4.8 copy.30
  600.5 0.7 copy.31
  (110 shorter events, 0.4 us)
Async XLA Ops:
  7.2 1.0 copy-start.10
  7.2 1.2 copy-start.39
  7.2 1.3 copy-start.40
  7.2 2.6 copy-start.12
  7.2 171.9 %all-gather.3.cloned.1.call-start = ((), (), s32[]{:S(2)}) async-start(), calls=%async_computation.1 | async-start | bytes 11796480 | tf_op jit(solution)/shard_map/all_gather | solution.py:54
  7.9 379.6 %all-gather.5.cloned.1.call-start = ((), (), s32[]{:S(2)}) async-start(), calls=%async_computation.2 | async-start | bytes 1966080 | tf_op jit(solution)/shard_map/all_gather | solution.py:95
  8.4 170.7 %copy-start = (bf16[1,128,1536]{1,2,0:T(8,128)(2,1)}, bf16[1,128,1536]{1,2,0:T(8,128)(2,1)S(1)}, u32[]{:S(2)}) copy-start(bf16[1,128,1536]{1,2,0:T(8,128)(2,1)S(1)} %copy.21) | copy-start | bytes 1179652
  9.8 176.1 %copy-start.37 = (f32[128]{0:T(128)}, f32[128]{0:T(128)S(1)}, u32[]{:S(2)}) copy-start(f32[128]{0:T(128)S(1)} %compare_convert_fusion) | copy-start | bytes 1540
  10.8 181.5 %copy-start.13 = (f32[1536]{0:T(1024)}, f32[1536]{0:T(1024)S(1)}, u32[]{:S(2)}) copy-start(f32[1536]{0:T(1024)S(1)} %get-tuple-element.38) | copy-start | bytes 18436
  10.8 181.5 %copy-start.15 = (f32[1536]{0:T(1024)}, f32[1536]{0:T(1024)S(1)}, u32[]{:S(2)}) copy-start(f32[1536]{0:T(1024)S(1)} %get-tuple-element.39) | copy-start | bytes 18436
  10.8 181.5 %copy-start.16 = (f32[1536]{0:T(1024)}, f32[1536]{0:T(1024)S(1)}, u32[]{:S(2)}) copy-start(f32[1536]{0:T(1024)S(1)} %get-tuple-element.40) | copy-start | bytes 18436
  10.8 181.5 %copy-start.17 = (f32[1536]{0:T(1024)}, f32[1536]{0:T(1024)S(1)}, u32[]{:S(2)}) copy-start(f32[1536]{0:T(1024)S(1)} %get-tuple-element.41) | copy-start | bytes 18436
  10.8 181.5 %copy-start.18 = (f32[1536]{0:T(1024)}, f32[1536]{0:T(1024)S(1)}, u32[]{:S(2)}) copy-start(f32[1536]{0:T(1024)S(1)} %get-tuple-element.42) | copy-start | bytes 18436
  10.8 181.5 %copy-start.19 = (f32[1536]{0:T(1024)}, f32[1536]{0:T(1024)S(1)}, u32[]{:S(2)}) copy-start(f32[1536]{0:T(1024)S(1)} %get-tuple-element.43) | copy-start | bytes 18436
  10.8 181.5 %copy-start.20 = (f32[1536]{0:T(1024)}, f32[1536]{0:T(1024)S(1)}, u32[]{:S(2)}) copy-start(f32[1536]{0:T(1024)S(1)} %get-tuple-element.44) | copy-start | bytes 18436
  10.8 181.5 %copy-start.21 = (f32[1536]{0:T(1024)}, f32[1536]{0:T(1024)S(1)}, u32[]{:S(2)}) copy-start(f32[1536]{0:T(1024)S(1)} %get-tuple-element.45) | copy-start | bytes 18436
  10.8 181.5 %copy-start.22 = (f32[1536]{0:T(1024)}, f32[1536]{0:T(1024)S(1)}, u32[]{:S(2)}) copy-start(f32[1536]{0:T(1024)S(1)} %get-tuple-element.46) | copy-start | bytes 18436
  10.8 181.5 %copy-start.23 = (f32[1536]{0:T(1024)}, f32[1536]{0:T(1024)S(1)}, u32[]{:S(2)}) copy-start(f32[1536]{0:T(1024)S(1)} %get-tuple-element.47) | copy-start | bytes 18436
  10.8 181.5 %copy-start.24 = (f32[1536]{0:T(1024)}, f32[1536]{0:T(1024)S(1)}, u32[]{:S(2)}) copy-start(f32[1536]{0:T(1024)S(1)} %get-tuple-element.48) | copy-start | bytes 18436
  10.8 181.5 %copy-start.25 = (f32[1536]{0:T(1024)}, f32[1536]{0:T(1024)S(1)}, u32[]{:S(2)}) copy-start(f32[1536]{0:T(1024)S(1)} %get-tuple-element.49) | copy-start | bytes 18436
  10.8 181.5 %copy-start.26 = (f32[1536]{0:T(1024)}, f32[1536]{0:T(1024)S(1)}, u32[]{:S(2)}) copy-start(f32[1536]{0:T(1024)S(1)} %get-tuple-element.50) | copy-start | bytes 18436
  186.2 95.4 %copy-start.1 = (bf16[1,128,1536]{2,1,0:T(8,128)(2,1)S(1)}, bf16[1,128,1536]{2,1,0:T(8,128)(2,1)}, u32[]{:S(2)}) copy-start(bf16[1,128,1536]{2,1,0:T(8,128)(2,1)} %param.15) | copy-start | bytes 1179652
  186.2 5.9 collective-permute-start.1
  187.7 4.5 collective-permute-start
  191.5 46.1 %copy-start.38 = (f32[128]{0:T(128)S(1)}, f32[128]{0:T(128)}, u32[]{:S(2)}) copy-start(f32[128]{0:T(128)} %copy-done.37) | copy-start | bytes 1540
  192.2 90.7 %copy-start.8 = (bf16[15,1536]{1,0:T(8,128)(2,1)}, bf16[15,1536]{1,0:T(8,128)(2,1)S(1)}, u32[]{:S(2)}) copy-start(bf16[15,1536]{1,0:T(8,128)(2,1)S(1)} %collective-permute-done.1) | copy-start | bytes 138244
  192.2 90.7 %copy-start.6 = (bf16[15,1536]{1,0:T(8,128)(2,1)}, bf16[15,1536]{1,0:T(8,128)(2,1)S(1)}, u32[]{:S(2)}) copy-start(bf16[15,1536]{1,0:T(8,128)(2,1)S(1)} %collective-permute-done) | copy-start | bytes 138244
  281.6 39.5 %copy-start.27 = (f32[1536]{0:T(1024)}, f32[1536]{0:T(1024)S(1)}, u32[]{:S(2)}) copy-start(f32[1536]{0:T(1024)S(1)} %get-tuple-element.77) | copy-start | bytes 18436
  324.9 6.6 %copy-start.14 = (f32[1536]{0:T(1024)S(1)}, f32[1536]{0:T(1024)}, u32[]{:S(2)}) copy-start(f32[1536]{0:T(1024)} %copy-done.13) | copy-start | bytes 18436
  324.9 6.6 %collective-permute-start.3 = (f32[15,1536]{1,0:T(8,128)S(1)}, f32[15,1536]{1,0:T(8,128)S(1)}, u32[]{:S(2)}, u32[]{:S(2)}) collective-permute-start(f32[15,1536]{1,0:T(8,128)S(1)} %get-tuple-element.81), channel_id=1, source_target_pairs={{1,0},{2,1},{3,2},{4,3},{5,4},{6,5},{7,6},{9,8},{10,9},{11,10},{12... | collective-permute-start | bytes 276488 | tf_op jit(solution)/shard_map/ppermute | solution.py:19
  326.2 5.3 collective-permute-start.2
  336.9 0.7 copy-start.2
  337.2 0.7 copy-start.4
  357.4 4.6 copy-start.7
  358.4 28.2 %all-to-all-start = ((bf16[4,2,49152]{2,1,0:T(2,128)(2,1)}), bf16[4,2,49152]{2,1,0:T(2,128)(2,1)S(1)}, u32[]{:S(2)}, u32[]{:S(2)}) async-start(bf16[4,2,49152]{2,1,0:T(2,128)(2,1)} %reshape.100), calls=%async_computation | async-start | bytes 1572864 | tf_op jit(solution)/shard_map/all_to_all | solution.py:92
  361.9 2.2 copy-start.9
  361.9 142.4 %all-reduce.6.cloned.1.call-start = ((), (), s32[]{:S(2)}) async-start(), calls=%async_computation.4 | async-start | bytes 393216 | tf_op jit(solution)/shard_map/psum | solution.py:85
  362.7 2.3 copy-start.36
  362.7 2.3 copy-start.35
  362.7 2.3 copy-start.34
  362.8 2.4 copy-start.33
  362.8 2.4 copy-start.32
  362.8 2.4 copy-start.31
  362.8 2.4 copy-start.30
  362.8 2.4 copy-start.29
  362.8 2.4 copy-start.28
  368.1 227.6 %all-reduce.4.cloned.1.call-start = ((), (), s32[]{:S(2)}) async-start(), calls=%async_computation.3 | async-start | bytes 9437184 | tf_op jit(solution)/shard_map/psum | solution.py:99
  391.9 1.0 copy-start.3
  391.9 1.1 copy-start.5
  504.4 96.1 %copy-start.11 = (f32[31,1536]{1,0:T(8,128)S(1)}, f32[31,1536]{1,0:T(8,128)}, u32[]{:S(2)}) copy-start(f32[31,1536]{1,0:T(8,128)} %all-reduce.6.cloned.1.call-done) | copy-start | bytes 571396
Sparse Core Ops, SparseCore 0:
  9.6 169.4 all-gather.2
  331.6 44.2 all-gather.4
  382.1 122.2 all-reduce.5
  508.1 87.5 all-reduce.3
where the time goes:
time: 609 us; the launch traced here: 608 us
  waiting for transfers between devices  384 us (63%)
  blocking collectives  121 us (20%)
  other arithmetic  39.5 us (6%)
  local copies, waits for them, and re-layouts  17.8 us (3%)
  matrix products  17.1 us (3%)
  between operations  15.4 us (3%)
  starting transfers between devices  12.8 us (2%)
    all_gather x1, waiting for transfers between devices, per_device(): weights = lax.all_gather(in_weight, 'dp', axis=0, tiled=True)  168 us
    psum x1, waiting for transfers between devices, per_device(): kernel_grad = lax.psum(kernel_part, ('dp', 'seq'))  105 us
    psum x1, waiting for transfers between devices, per_device(): weight_grad = lax.psum(local_rows, 'seq')  91.3 us
    psum x1, blocking collectives, per_device(): lax.psum(jnp.sum(centered * centered, axis=0), ('dp', 'seq')) / counted  42.5 us
    psum x1, blocking collectives, per_device(): lax.psum(jnp.sum(conv_out * valid_mask, axis=0), ('dp', 'seq')) / counted  40.2 us
    psum x1, blocking collectives, per_device(): lax.psum((jnp.sum(grad_shaped, axis=0), jnp.sum(grad_shaped * normed, axi...  38.3 us
    all_to_all x1, waiting for transfers between devices, per_device(): lax.all_to_all(grad_pre[None], 'dp', split_axis=2, concat_axis=0, tiled=T...  18.3 us
    unnamed x1, other arithmetic  17 us
  transfers between devices with their start and end apart: 9, of which 4 were waited for; matrix products, arithmetic and copies ran while one was open for 8% of the time, Pallas kernels for 0%

commit v1 on v0

--- a/solution.py
+++ b/solution.py
@@ -1,9 +1,338 @@
+import functools
+
 import jax
 import jax.numpy as jnp
 from jax import lax
+from jax.experimental import pallas as pl
+from jax.experimental.pallas import tpu as pltpu
 from jax.sharding import PartitionSpec as P
 
 EPS = 1e-05
+MESH = pl.DeviceIdType.MESH
+VM = pl.BlockSpec(memory_space=pltpu.VMEM)
+
+
+def at(d, s):
+    return {"dp": d, "seq": s}
+
+
+def greet(peers):
+    barrier = pltpu.get_barrier_semaphore()
+    for peer in peers:
+        pl.semaphore_signal(barrier, inc=1, device_id=peer, device_id_type=MESH)
+    pl.semaphore_wait(barrier, len(peers))
+
+
+def remote(src, dst, send, recv, peer):
+    return pltpu.make_async_remote_copy(
+        src_ref=src, dst_ref=dst, send_sem=send, recv_sem=recv, device_id=peer, device_id_type=MESH
+    )
+
+
+def ring_peers(me, count):
+    return [lax.rem(me + k, count) for k in range(1, count)]
+
+
+def merge(parts, stats):
+    if not stats:
+        return functools.reduce(lambda a, b: a + b, parts)
+    sums = [part[0:16] for part in parts]
+    squares = [part[16:32] for part in parts]
+    counts = [part[32:48] for part in parts]
+    total = functools.reduce(lambda a, b: a + b, sums)
+    count = functools.reduce(lambda a, b: a + b, counts)
+    mean = total / jnp.maximum(count, 1.0)
+    spread = functools.reduce(lambda a, b: a + b, squares)
+    for own, n in zip(sums, counts):
+        shift = own / jnp.maximum(n, 1.0) - mean
+        spread = spread + n * (shift * shift)
+    return jnp.concatenate([total, spread, count], axis=0)
+
+
+def sum_kernel(stats, dp_n, seq_n, x_ref, o_ref, near, far, mid, s1, r1, s2, r2):
+    d, s = lax.axis_index("dp"), lax.axis_index("seq")
+    plane = ring_peers(s, seq_n)
+    line = ring_peers(d, dp_n)
+    greet([at(d, j) for j in plane] + [at(j, s) for j in line])
+    for k, j in enumerate(plane):
+        remote(x_ref, near.at[s], s1.at[k], r1.at[s], at(d, j)).start()
+    near[s] = x_ref[...]
+    for k, j in enumerate(plane):
+        copy = remote(x_ref, near.at[j], s1.at[k], r1.at[j], at(d, j))
+        copy.wait_recv()
+        copy.wait_send()
+    mid[...] = merge([near[j] for j in range(seq_n)], stats)
+    for k, j in enumerate(line):
+        remote(mid, far.at[d], s2.at[k], r2.at[d], at(j, s)).start()
+    far[d] = mid[...]
+    for k, j in enumerate(line):
+        copy = remote(mid, far.at[j], s2.at[k], r2.at[j], at(j, s))
+        copy.wait_recv()
+        copy.wait_send()
+    o_ref[...] = merge([far[j] for j in range(dp_n)], stats)
+
+
+def sum_all(vectors, stats, collective_id):
+    dp_n, seq_n = lax.axis_size("dp"), lax.axis_size("seq")
+    blocks = vectors[0].shape[-1] // 128
+    stacked = jnp.stack([v.reshape(blocks, 128) for v in vectors])
+    stacked = jnp.pad(stacked, ((0, 0), (0, 16 - blocks), (0, 0)))
+    rows = 16 * len(vectors)
+    shape = (rows, 128)
+    out = pl.pallas_call(
+        functools.partial(sum_kernel, stats, dp_n, seq_n),
+        out_shape=jax.ShapeDtypeStruct(shape, jnp.float32),
+        in_specs=[VM],
+        out_specs=VM,
+        scratch_shapes=[
+            pltpu.VMEM((seq_n,) + shape, jnp.float32),
+            pltpu.VMEM((dp_n,) + shape, jnp.float32),
+            pltpu.VMEM(shape, jnp.float32),
+            pltpu.SemaphoreType.DMA((seq_n,)),
+            pltpu.SemaphoreType.DMA((seq_n,)),
+            pltpu.SemaphoreType.DMA((dp_n,)),
+            pltpu.SemaphoreType.DMA((dp_n,)),
+        ],
+        compiler_params=pltpu.CompilerParams(collective_id=collective_id, has_side_effects=True),
+    )(stacked.reshape(shape))
+    return out.reshape(len(vectors), 16, 128)[:, :blocks].reshape(len(vectors), blocks * 128)
+
+
+def square_at(s):
+    c, x, y = lax.rem(s, 2), lax.rem(s // 2, 2), s // 4
+    sx = (y * 2 + (1 - x)) * 2 + c
+    sy = ((1 - y) * 2 + x) * 2 + c
+    sd = ((1 - y) * 2 + (1 - x)) * 2 + c
+    sc = (y * 2 + x) * 2 + (1 - c)
+    return c, x, y, sx, sy, sd, sc
+
+
+def weights_kernel(w_ref, out, local, zs, zr, xs, xr, ys, yr, fs, fr, cs, cr):
+    d, s = lax.axis_index("dp"), lax.axis_index("seq")
+    c, x, y, sx, sy, sd, sc = square_at(s)
+    rows = w_ref.shape[1]
+    half = rows // 2
+    low, high = pl.ds(0, half), pl.ds(half, half)
+    line = [d + 1 - 2 * lax.rem(d, 2), 2 - d // 2, 3 - 3 * (d // 2)]
+    px, py, pc = at(d, sx), at(d, sy), at(d, sc)
+    greet([at(j, s) for j in line] + [px, py, pc])
+    for k, j in enumerate(line):
+        remote(w_ref.at[s], out.at[d, s], zs.at[k], zr.at[d], at(j, s)).start()
+    own = pltpu.make_async_copy(w_ref, out.at[d], local)
+    own.start()
+    pending = []
+    core = []
+
+    def to_core(k, n, ref, other):
+        copy = remote(ref, ref, cs.at[k, n], cr.at[k, n], pc)
+        copy.start()
+        pending.append(copy)
+        core.append(remote(other, other, cs.at[k, n], cr.at[k, n], pc))
+
+    cx, cy, cd = sx + 1 - 2 * c, sy + 1 - 2 * c, sd + 1 - 2 * c
+    for k, j in enumerate(line):
+        mine = out.at[j, s]
+        remote(mine, mine, zs.at[k], zr.at[j], at(j, s)).wait_recv()
+        for send, recv, peer in ((xs, xr, px), (ys, yr, py)):
+            copy = remote(mine, mine, send.at[k], recv.at[k], peer)
+            copy.start()
+            pending.append(copy)
+        to_core(k, 0, mine, out.at[j, sc])
+    for k, j in enumerate(line):
+        remote(out.at[j, sx], out.at[j, sx], xs.at[k], xr.at[k], px).wait_recv()
+        part = out.at[j, sx, low]
+        copy = remote(part, part, fs.at[k, 0], fr.at[k, 0], py)
+        copy.start()
+        pending.append(copy)
+        to_core(k, 1, out.at[j, sx], out.at[j, cx])
+        remote(out.at[j, sy], out.at[j, sy], ys.at[k], yr.at[k], py).wait_recv()
+        part = out.at[j, sy, high]
+        copy = remote(part, part, fs.at[k, 1], fr.at[k, 1], px)
+        copy.start()
+        pending.append(copy)
+        to_core(k, 2, out.at[j, sy], out.at[j, cy])
+    for k, j in enumerate(line):
+        part = out.at[j, sd, low]
+        remote(part, part, fs.at[k, 0], fr.at[k, 0], py).wait_recv()
+        to_core(k, 3, part, out.at[j, cd, low])
+        part = out.at[j, sd, high]
+        remote(part, part, fs.at[k, 1], fr.at[k, 1], px).wait_recv()
+        to_core(k, 4, part, out.at[j, cd, high])
+    for copy in core:
+        copy.wait_recv()
+    for copy in pending:
+        copy.wait_send()
+    for k, j in enumerate(line):
+        remote(w_ref.at[s], out.at[d, s], zs.at[k], zr.at[d], at(j, s)).wait_send()
+    own.wait()
+
+
+def gather_weights(in_weight):
+    dp_n, seq_n = lax.axis_size("dp"), lax.axis_size("seq")
+    rows, width = in_weight.shape
+    dma = pltpu.SemaphoreType.DMA
+    out = pl.pallas_call(
+        weights_kernel,
+        out_shape=jax.ShapeDtypeStruct((dp_n, seq_n, rows // seq_n, width), in_weight.dtype),
+        in_specs=[VM],
+        out_specs=pl.BlockSpec(memory_space=pl.ANY),
+        scratch_shapes=[dma(()), dma((3,)), dma((4,)), dma((3,)), dma((3,)), dma((3,)), dma((3,)),
+                        dma((3, 2)), dma((3, 2)), dma((3, 5)), dma((3, 5))],
+        compiler_params=pltpu.CompilerParams(collective_id=2, has_side_effects=True),
+    )(in_weight.reshape(seq_n, rows // seq_n, width))
+    return out.reshape(dp_n * rows, width)
+
+
+def grads_kernel(dp_n, seq_n, p_ref, kp_ref, o_ref, ko_ref, r0, acc, sa, sb, ra, rb, sa2, sb2, ra2,
+                 rb2, kb1, km, kb2, ws, wr, k1s, k1r, k2s, k2r, k3s, k3r):
+    d, s = lax.axis_index("dp"), lax.axis_index("seq")
+    c, x, y, sx, sy, sd, sc = square_at(s)
+    plane = ring_peers(s, seq_n)
+    line = ring_peers(d, dp_n)
+    px, py, pc = at(d, sx), at(d, sy), at(d, sc)
+    rows = p_ref.shape[0]
+    h, q, e, t = rows // 2, rows // 4, rows // 8, rows // 16
+
+    def span(start, size):
+        return pl.ds(pl.multiple_of(start, 16), size)
+
+    def each(size, fn):
+        @pl.loop(0, size // 16)
+        def _(i):
+            fn(pl.multiple_of(i * 16, 16))
+
+    greet([at(d, j) for j in plane] + [at(j, s) for j in line])
+    first = remote(p_ref.at[span((1 - c) * h, h)], r0, ws.at[0], wr.at[0], pc)
+    first.start()
+    for k, j in enumerate(plane):
+        remote(kp_ref.at[j], kb1.at[s], k1s.at[k], k1r.at[s], at(d, j)).start()
+    kb1[s] = kp_ref[s]
+    for k, j in enumerate(plane):
+        copy = remote(kp_ref.at[j], kb1.at[j], k1s.at[k], k1r.at[j], at(d, j))
+        copy.wait_recv()
+        copy.wait_send()
+    km[...] = merge([kb1[j] for j in range(seq_n)], False)
+    for k, j in enumerate(line):
+        remote(km, kb2.at[d], k2s.at[k], k2r.at[d], at(j, s)).start()
+    kb2[d] = km[...]
+    first.wait()
+
+    def add0(i):
+        acc[pl.ds(i, 16)] = p_ref[span(c * h + i, 16)] + r0[pl.ds(i, 16)]
+
+    each(h, add0)
+
+    def pack1(i):
+        sa[pl.ds(i, 16)] = acc[span((1 - x) * e + i, 16)].astype(jnp.bfloat16)
+        sb[pl.ds(i, 16)] = acc[span(q + (1 - y) * e + i, 16)].astype(jnp.bfloat16)
+
+    each(e, pack1)
+    one = remote(sa, ra, ws.at[1], wr.at[1], px)
+    two = remote(sb, rb, ws.at[2], wr.at[2], py)
+    one.start()
+    two.start()
+    for k, j in enumerate(line):
+        copy = remote(km, kb2.at[j], k2s.at[k], k2r.at[j], at(j, s))
+        copy.wait_recv()
+        copy.wait_send()
+    ko_ref[s] = merge([kb2[j] for j in range(dp_n)], False)
+    for k, j in enumerate(plane):
+        remote(ko_ref.at[s], ko_ref.at[s], k3s.at[k], k3r.at[s], at(d, j)).start()
+    one.wait()
+    two.wait()
+
+    def pack2(i):
+        away_a, away_b = (1 - y) * t + i, (1 - x) * t + i
+        sa2[pl.ds(i, 16)] = (
+            acc[span(x * e + away_a, 16)] + ra[span(away_a, 16)].astype(jnp.float32)
+        ).astype(jnp.bfloat16)
+        sb2[pl.ds(i, 16)] = (
+            acc[span(q + y * e + away_b, 16)] + rb[span(away_b, 16)].astype(jnp.float32)
+        ).astype(jnp.bfloat16)
+
+    each(t, pack2)
+    one = remote(sa2, ra2, ws.at[3], wr.at[3], py)
+    two = remote(sb2, rb2, ws.at[4], wr.at[4], px)
+    one.start()
+    two.start()
+    one.wait()
+    two.wait()
+
+    def last(i):
+        keep_a, keep_b = y * t + i, x * t + i
+        o_ref[span(c * h + x * e + keep_a, 16)] = (
+            acc[span(x * e + keep_a, 16)] + ra[span(keep_a, 16)].astype(jnp.float32)
+            + ra2[pl.ds(i, 16)].astype(jnp.float32)
+        ).astype(jnp.bfloat16)
+        o_ref[span(c * h + q + y * e + keep_b, 16)] = (
+            acc[span(q + y * e + keep_b, 16)] + rb[span(keep_b, 16)].astype(jnp.float32)
+            + rb2[pl.ds(i, 16)].astype(jnp.float32)
+        ).astype(jnp.bfloat16)
+
+    each(t, last)
+
+    def swap(mine, other, n, peer):
+        copy = remote(o_ref.at[mine], o_ref.at[mine], ws.at[n], wr.at[n], peer)
+        copy.start()
+        return copy, remote(o_ref.at[other], o_ref.at[other], ws.at[n], wr.at[n], peer)
+
+    def finish(pairs):
+        for copy, arrival in pairs:
+            arrival.wait_recv()
+        for copy, arrival in pairs:
+            copy.wait_send()
+
+    base = c * h
+    finish([
+        swap(span(base + x * e + y * t, t), span(base + x * e + (1 - y) * t, t), 5, py),
+        swap(span(base + q + y * e + x * t, t), span(base + q + y * e + (1 - x) * t, t), 6, px),
+    ])
+    finish([
+        swap(span(base + x * e, e), span(base + (1 - x) * e, e), 7, px),
+        swap(span(base + q + y * e, e), span(base + q + (1 - y) * e, e), 8, py),
+    ])
+    finish([swap(span(base, h), span((1 - c) * h, h), 9, pc)])
+    for k, j in enumerate(plane):
+        remote(ko_ref.at[j], ko_ref.at[j], k3s.at[k], k3r.at[j], at(d, j)).wait_recv()
+        remote(ko_ref.at[s], ko_ref.at[s], k3s.at[k], k3r.at[s], at(d, j)).wait_send()
+
+
+def sum_grads(partial, kernel_part):
+    dp_n, seq_n = lax.axis_size("dp"), lax.axis_size("seq")
+    rows, width = partial.shape
+    taps, channels = kernel_part.shape
+    packed = jnp.pad(kernel_part, ((0, 1), (0, 0))).reshape(seq_n, -1, 128)
+    block = packed.shape[1:]
+    dma = pltpu.SemaphoreType.DMA
+    bf = jnp.bfloat16
+    summed, taps_sum = pl.pallas_call(
+        functools.partial(grads_kernel, dp_n, seq_n),
+        out_shape=(
+            jax.ShapeDtypeStruct((rows, width), bf),
+            jax.ShapeDtypeStruct(packed.shape, jnp.float32),
+        ),
+        in_specs=[VM, VM],
+        out_specs=(VM, VM),
+        scratch_shapes=[
+            pltpu.VMEM((rows // 2, width), jnp.float32),
+            pltpu.VMEM((rows // 2, width), jnp.float32),
+            pltpu.VMEM((rows // 8, width), bf),
+            pltpu.VMEM((rows // 8, width), bf),
+            pltpu.VMEM((rows // 8, width), bf),
+            pltpu.VMEM((rows // 8, width), bf),
+            pltpu.VMEM((rows // 16, width), bf),
+            pltpu.VMEM((rows // 16, width), bf),
+            pltpu.VMEM((rows // 16, width), bf),
+            pltpu.VMEM((rows // 16, width), bf),
+            pltpu.VMEM((seq_n,) + block, jnp.float32),
+            pltpu.VMEM(block, jnp.float32),
+            pltpu.VMEM((dp_n,) + block, jnp.float32),
+            dma((10,)), dma((10,)),
+            dma((seq_n,)), dma((seq_n,)), dma((dp_n,)), dma((dp_n,)), dma((seq_n,)), dma((seq_n,)),
+        ],
+        compiler_params=pltpu.CompilerParams(collective_id=3, has_side_effects=True),
+    )(partial, packed)
+    return summed.astype(jnp.float32), taps_sum.reshape(taps + 1, channels)[:taps]
 
 
 def padded_2(cells, sides, width):
@@ -51,7 +380,11 @@
         :, None
     ]
     restored = restore(saved_codes[0], code_scales[0])
-    weights = lax.all_gather(in_weight, "dp", axis=0, tiled=True)
+    square = lax.axis_size("dp") == 4 and lax.axis_size("seq") == 8
+    if square:
+        weights = gather_weights(in_weight)
+    else:
+        weights = lax.all_gather(in_weight, "dp", axis=0, tiled=True)
     pre_act = lax.dot_general(
         restored, weights, (((1,), (1,)), ((), ())), preferred_element_type=jnp.float32
     )
@@ -60,9 +393,15 @@
     gated = (linear * gate_part * valid_mask).astype(jnp.bfloat16)
     gated_pad = padded_2(gated, (("seq", 0),), half_span)
     conv_out = depthwise(gated_pad, conv_kernel, frames)
-    mean_value = lax.psum(jnp.sum(conv_out * valid_mask, axis=0), ("dp", "seq")) / counted
-    centered = (conv_out - mean_value) * valid_mask
-    variance = lax.psum(jnp.sum(centered * centered, axis=0), ("dp", "seq")) / counted
+    own_sum = jnp.sum(conv_out * valid_mask, axis=0)
+    own_count = jnp.sum(valid_mask)
+    centered = (conv_out - own_sum / jnp.maximum(own_count, 1.0)) * valid_mask
+    own_square = jnp.sum(centered * centered, axis=0)
+    total, spread, _ = sum_all(
+        [own_sum, own_square, jnp.full_like(own_sum, own_count)], True, 0
+    )
+    mean_value = total / counted
+    variance = spread / counted
     inverse = lax.rsqrt(variance + EPS)
     normed = (conv_out - mean_value) * inverse
     shaped = bn_gain * normed + bn_shift
@@ -70,8 +409,8 @@
     grad_shaped = (
         out_grad[0].astype(jnp.float32) * valid_mask * smooth * (1.0 + shaped * (1.0 - smooth))
     )
-    shift_grad, gain_grad = lax.psum(
-        (jnp.sum(grad_shaped, axis=0), jnp.sum(grad_shaped * normed, axis=0)), ("dp", "seq")
+    shift_grad, gain_grad = sum_all(
+        [jnp.sum(grad_shaped, axis=0), jnp.sum(grad_shaped * normed, axis=0)], False, 1
     )
     grad_conv = (
         bn_gain * inverse * (grad_shaped - (shift_grad + normed * gain_grad) / counted) * valid_mask
@@ -82,7 +421,6 @@
             for offset in range(tap_count)
         ]
     )
-    kernel_grad = lax.psum(kernel_part, ("dp", "seq"))
     grad_pad = padded_2(grad_conv, (("seq", 0),), half_span)
     grad_gated = depthwise(grad_pad, conv_kernel[::-1], frames) * valid_mask
     grad_pre = jnp.concatenate(
@@ -96,7 +434,11 @@
         (((0, 1), (0, 1)), ((), ())),
         preferred_element_type=jnp.float32,
     )
-    weight_grad = lax.psum(local_rows, "seq")
+    if square:
+        weight_grad, kernel_grad = sum_grads(local_rows, kernel_part)
+    else:
+        weight_grad = lax.psum(local_rows, "seq")
+        kernel_grad = lax.psum(kernel_part, ("dp", "seq"))
     return (in_grad.astype(jnp.bfloat16)[None], weight_grad, kernel_grad, gain_grad, shift_grad)
 
 

time: 609 us -> 247 us (0.41)
  waiting for transfers between devices: 384 us -> 11.5 us
  Pallas kernels: 0 us -> 127 us
  blocking collectives: 121 us -> 0 us
    psum x2 -> x0, waiting for transfers between devices: 197 us -> none  [the longest x1 105 us: per_device(): kernel_grad = lax.psum(kernel_part, ('dp', 'seq'))]
    all_gather x1 -> x0, waiting for transfers between devices: 168 us -> none  [per_device(): weights = lax.all_gather(in_weight, 'dp', axis=0, tiled=True)]
    pallas_call x0 -> x4, Pallas kernels: none -> 127 us  [the longest x1 59.1 us: gather_weights(): pl.pallas_call(weights_kernel, out_shape=jax.ShapeDtypeStruct((dp_n, seq_...]
    psum x3 -> x0, blocking collectives: 121 us -> none  [the longest x1 42.5 us: per_device(): lax.psum(jnp.sum(centered * centered, axis=0), ('dp', 'seq')) / counted]
    all_to_all x1, waiting for transfers between devices: 18.3 us -> 11.5 us  [per_device(): lax.all_to_all(grad_pre[None], 'dp', split_axis=2, concat_axis=0, tiled=T...]
  transfers between devices with their start and end apart: 9 -> 6, of which waited for: 4 -> 1; matrix products, arithmetic and copies ran while one was open for 8% -> 23% of each run, Pallas kernels for 0% -> 11%
where the time goes in v1:
time: 247 us; the launch traced here: 246 us
  Pallas kernels  127 us (51%)
  other arithmetic  45.3 us (18%)
  between operations  17.2 us (7%)
  matrix products  17.1 us (7%)
  local copies, waits for them, and re-layouts  15.3 us (6%)
  starting transfers between devices  12.8 us (5%)
  waiting for transfers between devices  11.5 us (5%)
    pallas_call x1, Pallas kernels, gather_weights(): pl.pallas_call(weights_kernel, out_shape=jax.ShapeDtypeStruct((dp_n, seq_...  59.1 us
    pallas_call x1, Pallas kernels, sum_grads(): pl.pallas_call(functools.partial(grads_kernel, dp_n, seq_n), out_shape=(j...  39.9 us
    pallas_call x2, Pallas kernels, sum_all(): pl.pallas_call(functools.partial(sum_kernel, stats, dp_n, seq_n), out_sha...  27.5 us
    unnamed x1, other arithmetic  17 us
    all_to_all x1, waiting for transfers between devices, per_device(): lax.all_to_all(grad_pre[None], 'dp', split_axis=2, concat_axis=0, tiled=T...  11.5 us
    reduce_sum x4, other arithmetic, per_device(): jnp.sum(grad_conv * gated_pad[offset:offset + frames].astype(jnp.float32)...  7.7 us
    dot_general x1, matrix products, per_device(): lax.dot_general(restored, weights, (((1,), (1,)), ((), ())), preferred_el...  6.86 us
    ppermute x2, starting transfers between devices, padded_2(): lax.ppermute(tail, axis, [(i, (i + 1) % count) for i in range(ends)])  6.25 us
  transfers between devices with their start and end apart: 6, of which 1 were waited for; matrix products, arithmetic and copies ran while one was open for 23% of the time, Pallas kernels for 11%

profile of v1, /device:TPU:0, one launch (start us, length us, event | category | flops | bytes accessed | tf_op | source)
XLA Modules:
  0.0 245.7 jit_solution(1102988513626593962)
XLA Ops:
  7.2 0.0 all-gather.2.cloned.1.call-start
  7.2 59.1 %shard_map.119 = bf16[4,8,96,1536]{3,2,1,0:T(8,128)(2,1)} custom-call(bf16[8,96,1536]{2,1,0:T(8,128)(2,1)} %bitcast.67), custom_call_target="tpu_custom_call" | custom-call | tf_op jit(solution)/shard_map/pallas_call | solution.py:174
  66.3 0.2 copy.21
  66.6 0.1 multiply_convert_fusion.3
  66.7 0.0 copy-start.95
  66.7 6.9 %fusion.203 = f32[128,3072]{1,0:T(8,128)S(1)} fusion(bf16[128,1536]{0,1:T(8,128)(2,1)S(1)} %bitcast.68, bf16[3072,1536]{1,0:T(8,128)(2,1)} %bitcast.61), kind=kOutput, calls=%fused_computation.407 | convolution fusion | flops 1207959552 | bytes 11403264 | tf_op jit(solution)/shard_map/dot_general | solution.py:388
  73.6 0.6 fusion.195
  74.2 1.2 fusion.199
  75.4 0.2 multiply_convert_fusion.2
  75.7 1.4 collective-permute-start.1
  77.2 3.0 %collective-permute-start = (bf16[15,1536]{1,0:T(8,128)(2,1)S(1)}, bf16[15,1536]{1,0:T(8,128)(2,1)S(1)}, u32[]{:S(2)}, u32[]{:S(2)}) collective-permute-start(bf16[15,1536]{1,0:T(8,128)(2,1)S(1)} %get-tuple-element.86), channel_id=1, source_target_pairs={{0,1},{1,2},{2,3},{3,4},{4,5},{5,6},{6,7},{8,9},{9,10},{10,11},{11... | collective-permute-start | bytes 138248 | tf_op jit(solution)/shard_map/ppermute | solution.py:346
  80.2 0.1 fusion.159
  80.3 0.9 copy.23
  81.2 0.0 all-gather.2.cloned.1.call-update
  81.3 0.0 copy-start.47
  81.3 0.3 slice_reduce_fusion.30
  81.8 0.2 slice_reduce_fusion.29
  83.4 0.7 pad.27.clone
  84.1 0.6 copy-done.7
  84.7 0.0 copy-done.5
  84.8 6.2 %multiply_reduce_fusion.2 = (f32[1536]{0:T(1024)S(1)}, f32[128,1536]{1,0:T(8,128)S(1)}) fusion(f32[128]{0:T(128)} %copy-done.85, bf16[15,1536]{1,0:T(8,128)(2,1)} %copy-done.7, bf16[128,1536]{1,0:T(8,128)(2,1)S(1)} %multiply_convert_fusion.2, f32[1536]{0:T(1024)S(1)} %get-tuple-element.42, f32[1536]{0:T(1024)S(1)} %get-tuple-element.71, ...), kind=kLoop, calls=%fused_computation.320 | loop fusion | flops 36174336 | bytes 1468928 | tf_op jit(solution)/shard_map/reduce_sum | solution.py:396
  91.0 0.2 multiply_reduce_fusion.1
  91.2 0.1 maximum_maximum_fusion
  91.3 0.6 pad.12
  91.9 14.4 %shard_map.120 = f32[48,128]{1,0:T(8,128)} custom-call(f32[48,128]{1,0:T(8,128)} %bitcast.72), custom_call_target="tpu_custom_call" | custom-call | tf_op jit(solution)/shard_map/pallas_call | solution.py:82
  106.3 0.7 fusion.188
  107.0 1.3 fusion.197
  108.3 0.5 fusion.194
  109.0 0.6 select_maximum_fusion
  109.6 13.1 %shard_map.121 = f32[32,128]{1,0:T(8,128)} custom-call(f32[32,128]{1,0:T(8,128)} %bitcast.79), custom_call_target="tpu_custom_call" | custom-call | tf_op jit(solution)/shard_map/pallas_call | solution.py:82
  122.8 0.7 slice_bitcast_fusion.1
  123.9 4.0 %fusion.148 = (f32[1536]{0:T(1024)}, f32[1536]{0:T(1024)}, f32[1536]{0:T(1024)}, f32[1536]{0:T(1024)}, f32[1536]{0:T(1024)}, /*index=5*/f32[1536]{0:T(1024)}, f3...) fusion(bf16[15,1536]{1,0:T(8,128)(2,1)} %copy-done.7, ...), kind=kLoop, calls=%fused_computation.296 | loop fusion | flops 14535168 | bytes 2504196 | tf_op jit(solution)/shard_map/reduce_sum | solution.py:420
  127.9 1.3 collective-permute-start.3
  129.2 3.2 %collective-permute-start.2 = (f32[15,1536]{1,0:T(8,128)S(1)}, f32[15,1536]{1,0:T(8,128)S(1)}, u32[]{:S(2)}, u32[]{:S(2)}) collective-permute-start(f32[15,1536]{1,0:T(8,128)S(1)} %get-tuple-element.84), channel_id=1, source_target_pairs={{0,1},{1,2},{2,3},{3,4},{4,5},{5,6},{6,7},{8,9},{9,10},{10,11},{11... | collective-permute-start | bytes 276488 | tf_op jit(solution)/shard_map/ppermute | solution.py:346
  132.4 1.8 fusion.118
  134.3 0.6 stack.104
  134.9 0.6 stack.105
  135.4 0.6 stack.106
  136.0 0.6 stack.107
  136.6 0.6 stack.108
  137.3 0.6 stack.109
  138.2 3.8 %multiply_convert_fusion.1 = (bf16[128,1536]{1,0:T(8,128)(2,1)S(1)}, f32[128,1536]{1,0:T(8,128)S(1)}) fusion(f32[128,3072]{1,0:T(8,128)S(1)} %fusion.203, f32[128]{0:T(128)S(1)} %copy-done.87, f32[15,1536]{1,0:T(8,128)S(1)} %collective-permute-done.3, f32[128,1536]{1,0:T(8,128)S(1)} %get-tuple-element.75, f32[1536]{0:T(1024)S(1)} %copy-done.50, ...), kind=kLoop, calls=%fused_computation.315 | loop fusion | flops 19070976 | bytes 3127808 | tf_op jit(solution)/shard_map/convert.6
  142.0 0.3 multiply_convert_fusion
  142.3 0.4 copy-done.1
  142.7 0.3 copy-done.3
  143.1 0.1 pad_maximum_fusion.2
  143.1 1.9 copy.22
  145.0 0.5 broadcast.106
  145.6 17.0 %reduce.63 = bf16[3072,128]{1,0:T(8,128)(2,1)S(1)} reduce(bf16[3072,1,128]{2,1,0:T(2,128)(2,1)S(1)} %bitcast.63, bf16[]{:T(256)} %broadcast.106), dimensions={1}, to_apply=%bitcast.50.reduce_sub_computation | reduce | bytes 1572866
  162.5 1.0 reshape.174
  163.5 3.8 %all-to-all-start = ((bf16[4,2,49152]{2,1,0:T(2,128)(2,1)}), bf16[4,2,49152]{2,1,0:T(2,128)(2,1)S(1)}, u32[]{:S(2)}, u32[]{:S(2)}) async-start(bf16[4,2,49152]{2,1,0:T(2,128)(2,1)} %reshape.174), calls=%async_computation | async-start | bytes 1572864 | tf_op jit(solution)/shard_map/all_to_all | solution.py:430
  167.5 1.1 fusion.127
  168.8 0.8 fusion.147
  170.0 0.3 stack.135
  170.3 0.7 reshape.137.kp_ref
  171.0 5.8 %fusion = bf16[1,128,1536]{2,1,0:T(8,128)(2,1)} fusion(bf16[3072,1536]{1,0:T(8,128)(2,1)} %bitcast.62, bf16[128,1536]{1,0:T(8,128)(2,1)S(1)} %copy-done.4, bf16[128,1536]{1,0:T(8,128)(2,1)S(1)} %copy-done.2), kind=kOutput, calls=%fused_computation.30 | convolution fusion | flops 1209729024 | bytes 10616832 | tf_op jit(solution)/shard_map/dot_general | solution.py:429
  176.9 11.5 %all-to-all-done = bf16[4,2,49152]{2,1,0:T(2,128)(2,1)S(1)} async-done(((bf16[4,2,49152]{2,1,0:T(2,128)(2,1)}), bf16[4,2,49152]{2,1,0:T(2,128)(2,1)S(1)}, u32[]{:S(2)}, u32[]{:S(2)}) %all-to-all-start) | async-done | bytes 786464 | tf_op jit(solution)/shard_map/all_to_all | solution.py:430
  188.3 0.7 reshape.175
  189.1 0.1 copy.25
  189.2 0.0 all-gather.2.cloned.1.call-done
  189.2 4.4 %convolution_bitcast_fusion.p_ref = f32[768,1536]{1,0:T(8,128)} fusion(bf16[4,128,768]{1,2,0:T(8,128)(2,1)S(1)} %bitcast.66, bf16[4,128,1536]{2,1,0:T(8,128)(2,1)} %all-gather.2.cloned.1.call-done), kind=kOutput, calls=%fused_computation.28 | convolution fusion | flops 1207959552 | bytes 7077888 | tf_op jit(solution)/shard_map/dot_general | solution.py:431
  193.6 39.9 %shard_map.122 = (bf16[768,1536]{1,0:T(8,128)(2,1)}, f32[8,48,128]{2,1,0:T(8,128)}) custom-call(f32[768,1536]{1,0:T(8,128)} %convolution_bitcast_fusion.p_ref, f32[8,48,128]{2,1,0:T(8,128)} %reshape.137.kp_ref), custom_call_target="tpu_custom_call" | custom-call | tf_op jit(solution)/shard_map/pallas_call | solution.py:308
  233.6 4.5 %convert_element_type.238 = f32[768,1536]{1,0:T(8,128)} convert(bf16[768,1536]{1,0:T(8,128)(2,1)} %get-tuple-element.7) | non-fusion elementwise | flops 1179648 | bytes 7077888 | tf_op jit(solution)/shard_map/convert_element_type | solution.py:335
  238.1 0.7 reshape.138
  (220 shorter events, 0.6 us)
Async XLA Ops:
  7.2 182.0 %all-gather.2.cloned.1.call-start = ((), (), s32[]{:S(2)}) async-start(), calls=%async_computation.1 | async-start | bytes 1966080 | tf_op jit(solution)/shard_map/all_gather | solution.py:433
  7.2 59.1 %copy-start.94 = (f32[1,12,128]{2,0,1:T(1,128)S(1)}, f32[1,12,128]{2,0,1:T(1,128)}, u32[]{:S(2)}) copy-start(f32[1,12,128]{2,0,1:T(1,128)} %param.9) | copy-start | bytes 18436
  7.2 59.1 %copy-start.9 = (bf16[1,128,1536]{2,1,0:T(8,128)(2,1)S(1)}, bf16[1,128,1536]{2,1,0:T(8,128)(2,1)}, u32[]{:S(2)}) copy-start(bf16[1,128,1536]{2,1,0:T(8,128)(2,1)} %param.8) | copy-start | bytes 1179652
  75.7 8.4 %collective-permute-start.1 = (bf16[15,1536]{1,0:T(8,128)(2,1)S(1)}, bf16[15,1536]{1,0:T(8,128)(2,1)S(1)}, u32[]{:S(2)}, u32[]{:S(2)}) collective-permute-start(bf16[15,1536]{1,0:T(8,128)(2,1)S(1)} %get-tuple-element.87), channel_id=1, source_target_pairs={{1,0},{2,1},{3,2},{4,3},{5,4},{6,5},{7,6},{9,8},{10,9},{11,10},{12... | collective-permute-start | bytes 138248 | tf_op jit(solution)/shard_map/ppermute | solution.py:348
  77.2 7.0 %collective-permute-start = (bf16[15,1536]{1,0:T(8,128)(2,1)S(1)}, bf16[15,1536]{1,0:T(8,128)(2,1)S(1)}, u32[]{:S(2)}, u32[]{:S(2)}) collective-permute-start(bf16[15,1536]{1,0:T(8,128)(2,1)S(1)} %get-tuple-element.86), channel_id=1, source_target_pairs={{0,1},{1,2},{2,3},{3,4},{4,5},{5,6},{6,7},{8,9},{9,10},{10,11},{11... | collective-permute-start | bytes 138248 | tf_op jit(solution)/shard_map/ppermute | solution.py:346
  81.3 25.8 %copy-start.47 = (f32[1536]{0:T(1024)S(1)}, f32[1536]{0:T(1024)}, u32[]{:S(2)}) copy-start(f32[1536]{0:T(1024)} %param.13) | copy-start | bytes 18436
  81.3 27.1 %copy-start = (bf16[1,128,1536]{2,1,0:T(8,128)(2,1)S(1)}, bf16[1,128,1536]{2,1,0:T(8,128)(2,1)}, u32[]{:S(2)}) copy-start(bf16[1,128,1536]{2,1,0:T(8,128)(2,1)} %param.15) | copy-start | bytes 1179652
  81.3 27.1 %copy-start.73 = (f32[1536]{0:T(1024)S(1)}, f32[1536]{0:T(1024)}, u32[]{:S(2)}) copy-start(f32[1536]{0:T(1024)} %param.14) | copy-start | bytes 18436
  81.6 27.2 %copy-start.12 = (f32[1536]{0:T(1024)}, f32[1536]{0:T(1024)S(1)}, u32[]{:S(2)}) copy-start(f32[1536]{0:T(1024)S(1)} %get-tuple-element.44) | copy-start | bytes 18436
  81.6 27.2 %copy-start.14 = (f32[1536]{0:T(1024)}, f32[1536]{0:T(1024)S(1)}, u32[]{:S(2)}) copy-start(f32[1536]{0:T(1024)S(1)} %get-tuple-element.45) | copy-start | bytes 18436
  81.6 27.2 %copy-start.16 = (f32[1536]{0:T(1024)}, f32[1536]{0:T(1024)S(1)}, u32[]{:S(2)}) copy-start(f32[1536]{0:T(1024)S(1)} %get-tuple-element.46) | copy-start | bytes 18436
  81.6 27.2 %copy-start.18 = (f32[1536]{0:T(1024)}, f32[1536]{0:T(1024)S(1)}, u32[]{:S(2)}) copy-start(f32[1536]{0:T(1024)S(1)} %get-tuple-element.47) | copy-start | bytes 18436
  81.7 27.2 %copy-start.20 = (f32[1536]{0:T(1024)}, f32[1536]{0:T(1024)S(1)}, u32[]{:S(2)}) copy-start(f32[1536]{0:T(1024)S(1)} %get-tuple-element.48) | copy-start | bytes 18436
  81.7 27.2 %copy-start.22 = (f32[1536]{0:T(1024)}, f32[1536]{0:T(1024)S(1)}, u32[]{:S(2)}) copy-start(f32[1536]{0:T(1024)S(1)} %get-tuple-element.49) | copy-start | bytes 18436
  81.7 27.2 %copy-start.24 = (f32[1536]{0:T(1024)}, f32[1536]{0:T(1024)S(1)}, u32[]{:S(2)}) copy-start(f32[1536]{0:T(1024)S(1)} %get-tuple-element.50) | copy-start | bytes 18436
  81.7 27.2 %copy-start.26 = (f32[1536]{0:T(1024)}, f32[1536]{0:T(1024)S(1)}, u32[]{:S(2)}) copy-start(f32[1536]{0:T(1024)S(1)} %get-tuple-element.51) | copy-start | bytes 18436
  81.7 27.2 %copy-start.28 = (f32[1536]{0:T(1024)}, f32[1536]{0:T(1024)S(1)}, u32[]{:S(2)}) copy-start(f32[1536]{0:T(1024)S(1)} %get-tuple-element.52) | copy-start | bytes 18436
  81.7 27.2 %copy-start.30 = (f32[1536]{0:T(1024)}, f32[1536]{0:T(1024)S(1)}, u32[]{:S(2)}) copy-start(f32[1536]{0:T(1024)S(1)} %get-tuple-element.53) | copy-start | bytes 18436
  81.7 27.2 %copy-start.32 = (f32[1536]{0:T(1024)}, f32[1536]{0:T(1024)S(1)}, u32[]{:S(2)}) copy-start(f32[1536]{0:T(1024)S(1)} %get-tuple-element.54) | copy-start | bytes 18436
  81.7 27.2 %copy-start.34 = (f32[1536]{0:T(1024)}, f32[1536]{0:T(1024)S(1)}, u32[]{:S(2)}) copy-start(f32[1536]{0:T(1024)S(1)} %get-tuple-element.55) | copy-start | bytes 18436
  81.7 27.2 %copy-start.36 = (f32[1536]{0:T(1024)}, f32[1536]{0:T(1024)S(1)}, u32[]{:S(2)}) copy-start(f32[1536]{0:T(1024)S(1)} %get-tuple-element.56) | copy-start | bytes 18436
  81.7 27.2 %copy-start.38 = (f32[1536]{0:T(1024)}, f32[1536]{0:T(1024)S(1)}, u32[]{:S(2)}) copy-start(f32[1536]{0:T(1024)S(1)} %get-tuple-element.57) | copy-start | bytes 18436
  81.8 27.2 %copy-start.40 = (f32[1536]{0:T(1024)}, f32[1536]{0:T(1024)S(1)}, u32[]{:S(2)}) copy-start(f32[1536]{0:T(1024)S(1)} %get-tuple-element.58) | copy-start | bytes 18436
  81.8 27.2 %copy-start.42 = (f32[1536]{0:T(1024)}, f32[1536]{0:T(1024)S(1)}, u32[]{:S(2)}) copy-start(f32[1536]{0:T(1024)S(1)} %get-tuple-element.59) | copy-start | bytes 18436
  81.8 27.2 %copy-start.44 = (f32[1536]{0:T(1024)}, f32[1536]{0:T(1024)S(1)}, u32[]{:S(2)}) copy-start(f32[1536]{0:T(1024)S(1)} %get-tuple-element.60) | copy-start | bytes 18436
  82.0 27.0 %copy-start.49 = (f32[1536]{0:T(1024)}, f32[1536]{0:T(1024)S(1)}, u32[]{:S(2)}) copy-start(f32[1536]{0:T(1024)S(1)} %get-tuple-element.61) | copy-start | bytes 18436
  82.0 27.0 %copy-start.51 = (f32[1536]{0:T(1024)}, f32[1536]{0:T(1024)S(1)}, u32[]{:S(2)}) copy-start(f32[1536]{0:T(1024)S(1)} %get-tuple-element.62) | copy-start | bytes 18436
  82.0 41.5 %copy-start.53 = (f32[1536]{0:T(1024)}, f32[1536]{0:T(1024)S(1)}, u32[]{:S(2)}) copy-start(f32[1536]{0:T(1024)S(1)} %get-tuple-element.63) | copy-start | bytes 18436
  82.0 41.5 %copy-start.55 = (f32[1536]{0:T(1024)}, f32[1536]{0:T(1024)S(1)}, u32[]{:S(2)}) copy-start(f32[1536]{0:T(1024)S(1)} %get-tuple-element.64) | copy-start | bytes 18436
  82.0 41.5 %copy-start.57 = (f32[1536]{0:T(1024)}, f32[1536]{0:T(1024)S(1)}, u32[]{:S(2)}) copy-start(f32[1536]{0:T(1024)S(1)} %get-tuple-element.65) | copy-start | bytes 18436
  82.0 41.5 %copy-start.59 = (f32[1536]{0:T(1024)}, f32[1536]{0:T(1024)S(1)}, u32[]{:S(2)}) copy-start(f32[1536]{0:T(1024)S(1)} %get-tuple-element.66) | copy-start | bytes 18436
  82.0 41.5 %copy-start.61 = (f32[1536]{0:T(1024)}, f32[1536]{0:T(1024)S(1)}, u32[]{:S(2)}) copy-start(f32[1536]{0:T(1024)S(1)} %get-tuple-element.67) | copy-start | bytes 18436
  82.1 41.5 %copy-start.63 = (f32[1536]{0:T(1024)}, f32[1536]{0:T(1024)S(1)}, u32[]{:S(2)}) copy-start(f32[1536]{0:T(1024)S(1)} %get-tuple-element.68) | copy-start | bytes 18436
  82.1 41.5 %copy-start.65 = (f32[1536]{0:T(1024)}, f32[1536]{0:T(1024)S(1)}, u32[]{:S(2)}) copy-start(f32[1536]{0:T(1024)S(1)} %get-tuple-element.69) | copy-start | bytes 18436
  82.1 41.5 %copy-start.67 = (f32[1536]{0:T(1024)}, f32[1536]{0:T(1024)S(1)}, u32[]{:S(2)}) copy-start(f32[1536]{0:T(1024)S(1)} %get-tuple-element.70) | copy-start | bytes 18436
  82.1 41.5 %copy-start.69 = (f32[1536]{0:T(1024)}, f32[1536]{0:T(1024)S(1)}, u32[]{:S(2)}) copy-start(f32[1536]{0:T(1024)S(1)} %get-tuple-element.71) | copy-start | bytes 18436
  82.1 41.5 %copy-start.71 = (f32[1536]{0:T(1024)}, f32[1536]{0:T(1024)S(1)}, u32[]{:S(2)}) copy-start(f32[1536]{0:T(1024)S(1)} %get-tuple-element.72) | copy-start | bytes 18436
  107.0 16.6 %copy-start.46 = (f32[1536]{0:T(1024)}, f32[1536]{0:T(1024)S(1)}, u32[]{:S(2)}) copy-start(f32[1536]{0:T(1024)S(1)} %fusion.188) | copy-start | bytes 18436
  108.3 15.3 %copy-start.48 = (f32[1536]{0:T(1024)}, f32[1536]{0:T(1024)S(1)}, u32[]{:S(2)}) copy-start(f32[1536]{0:T(1024)S(1)} %get-tuple-element.79) | copy-start | bytes 18436
  123.6 14.3 %copy-start.13 = (f32[1536]{0:T(1024)S(1)}, f32[1536]{0:T(1024)}, u32[]{:S(2)}) copy-start(f32[1536]{0:T(1024)} %copy-done.12) | copy-start | bytes 18436
  123.6 14.3 %copy-start.15 = (f32[1536]{0:T(1024)S(1)}, f32[1536]{0:T(1024)}, u32[]{:S(2)}) copy-start(f32[1536]{0:T(1024)} %copy-done.14) | copy-start | bytes 18436
  123.6 14.3 %copy-start.17 = (f32[1536]{0:T(1024)S(1)}, f32[1536]{0:T(1024)}, u32[]{:S(2)}) copy-start(f32[1536]{0:T(1024)} %copy-done.16) | copy-start | bytes 18436
  123.6 14.3 %copy-start.19 = (f32[1536]{0:T(1024)S(1)}, f32[1536]{0:T(1024)}, u32[]{:S(2)}) copy-start(f32[1536]{0:T(1024)} %copy-done.18) | copy-start | bytes 18436
  123.6 14.3 %copy-start.21 = (f32[1536]{0:T(1024)S(1)}, f32[1536]{0:T(1024)}, u32[]{:S(2)}) copy-start(f32[1536]{0:T(1024)} %copy-done.20) | copy-start | bytes 18436
  123.6 14.3 %copy-start.23 = (f32[1536]{0:T(1024)S(1)}, f32[1536]{0:T(1024)}, u32[]{:S(2)}) copy-start(f32[1536]{0:T(1024)} %copy-done.22) | copy-start | bytes 18436
  123.7 14.3 %copy-start.25 = (f32[1536]{0:T(1024)S(1)}, f32[1536]{0:T(1024)}, u32[]{:S(2)}) copy-start(f32[1536]{0:T(1024)} %copy-done.24) | copy-start | bytes 18436
  123.7 14.3 %copy-start.27 = (f32[1536]{0:T(1024)S(1)}, f32[1536]{0:T(1024)}, u32[]{:S(2)}) copy-start(f32[1536]{0:T(1024)} %copy-done.26) | copy-start | bytes 18436
  123.7 14.3 %copy-start.29 = (f32[1536]{0:T(1024)S(1)}, f32[1536]{0:T(1024)}, u32[]{:S(2)}) copy-start(f32[1536]{0:T(1024)} %copy-done.28) | copy-start | bytes 18436
  123.7 14.3 %copy-start.31 = (f32[1536]{0:T(1024)S(1)}, f32[1536]{0:T(1024)}, u32[]{:S(2)}) copy-start(f32[1536]{0:T(1024)} %copy-done.30) | copy-start | bytes 18436
  123.7 14.3 %copy-start.33 = (f32[1536]{0:T(1024)S(1)}, f32[1536]{0:T(1024)}, u32[]{:S(2)}) copy-start(f32[1536]{0:T(1024)} %copy-done.32) | copy-start | bytes 18436
  123.7 14.3 %copy-start.35 = (f32[1536]{0:T(1024)S(1)}, f32[1536]{0:T(1024)}, u32[]{:S(2)}) copy-start(f32[1536]{0:T(1024)} %copy-done.34) | copy-start | bytes 18436
  123.7 14.3 %copy-start.37 = (f32[1536]{0:T(1024)S(1)}, f32[1536]{0:T(1024)}, u32[]{:S(2)}) copy-start(f32[1536]{0:T(1024)} %copy-done.36) | copy-start | bytes 18436
  123.7 14.3 %copy-start.39 = (f32[1536]{0:T(1024)S(1)}, f32[1536]{0:T(1024)}, u32[]{:S(2)}) copy-start(f32[1536]{0:T(1024)} %copy-done.38) | copy-start | bytes 18436
  123.7 14.3 %copy-start.41 = (f32[1536]{0:T(1024)S(1)}, f32[1536]{0:T(1024)}, u32[]{:S(2)}) copy-start(f32[1536]{0:T(1024)} %copy-done.40) | copy-start | bytes 18436
  123.7 14.3 %copy-start.43 = (f32[1536]{0:T(1024)S(1)}, f32[1536]{0:T(1024)}, u32[]{:S(2)}) copy-start(f32[1536]{0:T(1024)} %copy-done.42) | copy-start | bytes 18436
  123.8 14.3 %copy-start.45 = (f32[1536]{0:T(1024)S(1)}, f32[1536]{0:T(1024)}, u32[]{:S(2)}) copy-start(f32[1536]{0:T(1024)} %copy-done.44) | copy-start | bytes 18436
  123.8 14.3 %copy-start.50 = (f32[1536]{0:T(1024)S(1)}, f32[1536]{0:T(1024)}, u32[]{:S(2)}) copy-start(f32[1536]{0:T(1024)} %copy-done.49) | copy-start | bytes 18436
  123.8 14.3 %copy-start.52 = (f32[1536]{0:T(1024)S(1)}, f32[1536]{0:T(1024)}, u32[]{:S(2)}) copy-start(f32[1536]{0:T(1024)} %copy-done.51) | copy-start | bytes 18436
  123.8 14.3 %copy-start.54 = (f32[1536]{0:T(1024)S(1)}, f32[1536]{0:T(1024)}, u32[]{:S(2)}) copy-start(f32[1536]{0:T(1024)} %copy-done.53) | copy-start | bytes 18436
  123.8 14.3 %copy-start.56 = (f32[1536]{0:T(1024)S(1)}, f32[1536]{0:T(1024)}, u32[]{:S(2)}) copy-start(f32[1536]{0:T(1024)} %copy-done.55) | copy-start | bytes 18436
  123.8 14.3 %copy-start.58 = (f32[1536]{0:T(1024)S(1)}, f32[1536]{0:T(1024)}, u32[]{:S(2)}) copy-start(f32[1536]{0:T(1024)} %copy-done.57) | copy-start | bytes 18436
  127.9 10.0 %collective-permute-start.3 = (f32[15,1536]{1,0:T(8,128)S(1)}, f32[15,1536]{1,0:T(8,128)S(1)}, u32[]{:S(2)}, u32[]{:S(2)}) collective-permute-start(f32[15,1536]{1,0:T(8,128)S(1)} %get-tuple-element.85), channel_id=1, source_target_pairs={{1,0},{2,1},{3,2},{4,3},{5,4},{6,5},{7,6},{9,8},{10,9},{11,10},{12... | collective-permute-start | bytes 276488 | tf_op jit(solution)/shard_map/ppermute | solution.py:348
  129.2 8.7 %collective-permute-start.2 = (f32[15,1536]{1,0:T(8,128)S(1)}, f32[15,1536]{1,0:T(8,128)S(1)}, u32[]{:S(2)}, u32[]{:S(2)}) collective-permute-start(f32[15,1536]{1,0:T(8,128)S(1)} %get-tuple-element.84), channel_id=1, source_target_pairs={{0,1},{1,2},{2,3},{3,4},{4,5},{5,6},{6,7},{8,9},{9,10},{10,11},{11... | collective-permute-start | bytes 276488 | tf_op jit(solution)/shard_map/ppermute | solution.py:346
  163.5 24.8 %all-to-all-start = ((bf16[4,2,49152]{2,1,0:T(2,128)(2,1)}), bf16[4,2,49152]{2,1,0:T(2,128)(2,1)S(1)}, u32[]{:S(2)}, u32[]{:S(2)}) async-start(bf16[4,2,49152]{2,1,0:T(2,128)(2,1)} %reshape.174), calls=%async_computation | async-start | bytes 1572864 | tf_op jit(solution)/shard_map/all_to_all | solution.py:430
  (38 other events, 217.8 us)
Sparse Core Ops, SparseCore 0:
  81.4 41.7 all-gather.1

commit v2 on v1

--- a/solution.py
+++ b/solution.py
@@ -33,69 +33,220 @@
     return [lax.rem(me + k, count) for k in range(1, count)]
 
 
-def merge(parts, stats):
-    if not stats:
-        return functools.reduce(lambda a, b: a + b, parts)
-    sums = [part[0:16] for part in parts]
-    squares = [part[16:32] for part in parts]
-    counts = [part[32:48] for part in parts]
-    total = functools.reduce(lambda a, b: a + b, sums)
+def total_of(parts):
+    return functools.reduce(lambda a, b: a + b, parts)
+
+
+def merge_moments(parts, counts):
     count = functools.reduce(lambda a, b: a + b, counts)
+    total = total_of([part[0:1] for part in parts])
     mean = total / jnp.maximum(count, 1.0)
-    spread = functools.reduce(lambda a, b: a + b, squares)
-    for own, n in zip(sums, counts):
-        shift = own / jnp.maximum(n, 1.0) - mean
+    spread = total_of([part[1:2] for part in parts])
+    for part, n in zip(parts, counts):
+        shift = part[0:1] / jnp.maximum(n, 1.0) - mean
         spread = spread + n * (shift * shift)
-    return jnp.concatenate([total, spread, count], axis=0)
-
-
-def sum_kernel(stats, dp_n, seq_n, x_ref, o_ref, near, far, mid, s1, r1, s2, r2):
+    return total, spread
+
+
+def middle_kernel(dp_n, seq_n, pre_ref, len_ref, taps_ref, gain_ref, bias_ref, up_ref,
+                  cols_ref, kp_ref, gg_ref, sg_ref, gpre,
+                  gp, gcp, co, gs, hs, hr, near, far, st, mid, near2, far2, st2, mid2,
+                  h_s, h_r, g_s, g_r, s1, r1, s2, r2, s3, r3, s4, r4, as_, ar_):
     d, s = lax.axis_index("dp"), lax.axis_index("seq")
+    frames, width = up_ref.shape
+    taps = taps_ref.shape[0]
     plane = ring_peers(s, seq_n)
     line = ring_peers(d, dp_n)
+    left, right = lax.rem(s + seq_n - 1, seq_n), lax.rem(s + 1, seq_n)
+    length = len_ref[d]
+    lengths = [len_ref[g] for g in range(dp_n)]
+    counted = functools.reduce(lambda a, b: a + b, lengths).astype(jnp.float32)
+
+    def share(j):
+        return jnp.clip(length - j * frames, 0, frames).astype(jnp.float32)
+
+    own_count = share(s)
+    row = lax.broadcasted_iota(jnp.int32, (frames, 1), 0) + s * frames
+    mask = jnp.broadcast_to((row < length).astype(jnp.float32), (frames, 128))
+    keep_left = jnp.where(s == 0, 0.0, 1.0).astype(jnp.float32)
+    keep_right = jnp.where(s == seq_n - 1, 0.0, 1.0).astype(jnp.float32)
+    body = pl.ds(16, frames)
+    tail = frames + 16
+
+    def blocks(fn):
+        @pl.loop(0, width // 128)
+        def _(i):
+            fn(pl.ds(pl.multiple_of(i * 128, 128), 128),
+               pl.ds(pl.multiple_of(width + i * 128, 128), 128))
+
+    def gate(a, b):
+        g = jax.nn.sigmoid(pre_ref[:, b])
+        value = (pre_ref[:, a] * g * mask).astype(jnp.bfloat16)
+        gp[body, a] = value.astype(jnp.float32)
+        hs[0, :, a] = value[0:16]
+        hs[1, :, a] = value[frames - 16 : frames]
+
+    blocks(gate)
     greet([at(d, j) for j in plane] + [at(j, s) for j in line])
-    for k, j in enumerate(plane):
-        remote(x_ref, near.at[s], s1.at[k], r1.at[s], at(d, j)).start()
-    near[s] = x_ref[...]
-    for k, j in enumerate(plane):
-        copy = remote(x_ref, near.at[j], s1.at[k], r1.at[j], at(d, j))
+    to_left = remote(hs.at[0], hr.at[1], h_s.at[0], h_r.at[1], at(d, left))
+    to_right = remote(hs.at[1], hr.at[0], h_s.at[1], h_r.at[0], at(d, right))
+    to_left.start()
+    to_right.start()
+    to_left.wait()
+    to_right.wait()
+
+    def conv(a, b):
+        gp[0:16, a] = hr[0, :, a].astype(jnp.float32) * keep_left
+        gp[tail : tail + 16, a] = hr[1, :, a].astype(jnp.float32) * keep_right
+        out = taps_ref[0:1, a] * gp[1 : 1 + frames, a]
+        for k in range(1, taps):
+            out = out + taps_ref[k : k + 1, a] * gp[k + 1 : k + 1 + frames, a]
+        co[:, a] = out
+        total = jnp.sum(out * mask, axis=0, keepdims=True)
+        centered = (out - total / jnp.maximum(own_count, 1.0)) * mask
+        st[0:1, a] = total
+        st[1:2, a] = jnp.sum(centered * centered, axis=0, keepdims=True)
+
+    blocks(conv)
+
+    def exchange(mine, slots, me, peers, where, send, recv):
+        for k, j in enumerate(peers):
+            remote(mine, slots.at[me], send.at[k], recv.at[me], where(j)).start()
+        slots[me] = mine[...]
+        for k, j in enumerate(peers):
+            copy = remote(mine, slots.at[j], send.at[k], recv.at[j], where(j))
+            copy.wait_recv()
+            copy.wait_send()
+
+    exchange(st, near, s, plane, lambda j: at(d, j), s1, r1)
+    total, spread = merge_moments([near[j] for j in range(seq_n)], [share(j) for j in range(seq_n)])
+    mid[0:1] = total
+    mid[1:2] = spread
+    exchange(mid, far, d, line, lambda j: at(j, s), s2, r2)
+    total, spread = merge_moments(
+        [far[j] for j in range(dp_n)], [n.astype(jnp.float32) for n in lengths]
+    )
+    mid[0:1] = total / counted
+    mid[1:2] = lax.rsqrt(spread / counted + EPS)
+
+    def shape(a, b):
+        normed = (co[:, a] - mid[0:1, a]) * mid[1:2, a]
+        shaped = gain_ref[:, a] * normed + bias_ref[:, a]
+        smooth = jax.nn.sigmoid(shaped)
+        grad = up_ref[:, a].astype(jnp.float32) * mask * smooth * (1.0 + shaped * (1.0 - smooth))
+        co[:, a] = normed
+        gs[:, a] = grad
+        st2[0:1, a] = jnp.sum(grad, axis=0, keepdims=True)
+        st2[1:2, a] = jnp.sum(grad * normed, axis=0, keepdims=True)
+
+    blocks(shape)
+    exchange(st2, near2, s, plane, lambda j: at(d, j), s3, r3)
+    mid2[...] = total_of([near2[j] for j in range(seq_n)])
+    exchange(mid2, far2, d, line, lambda j: at(j, s), s4, r4)
+    both = total_of([far2[j] for j in range(dp_n)])
+    sg_ref[...] = both[0:1]
+    gg_ref[...] = both[1:2]
+
+    def back(a, b):
+        scale = gain_ref[:, a] * mid[1:2, a]
+        gcp[body, a] = (
+            scale * (gs[:, a] - (sg_ref[:, a] + co[:, a] * gg_ref[:, a]) / counted) * mask
+        )
+
+    blocks(back)
+    to_left = remote(
+        gcp.at[pl.ds(16, 16)], gcp.at[pl.ds(tail, 16)], g_s.at[0], g_r.at[1], at(d, left)
+    )
+    to_right = remote(
+        gcp.at[pl.ds(tail - 16, 16)], gcp.at[pl.ds(0, 16)], g_s.at[1], g_r.at[0], at(d, right)
+    )
+    to_left.start()
+    to_right.start()
+    to_left.wait()
+    to_right.wait()
+    gcp[0:16] = gcp[0:16] * keep_left
+    gcp[tail : tail + 16] = gcp[tail : tail + 16] * keep_right
+    part = 2 * width // dp_n
+
+    def unconv(half):
+        def fn(i, a, b, a_out, b_out):
+            out = taps_ref[0:1, a] * gcp[taps : taps + frames, a]
+            for k in range(1, taps):
+                out = out + taps_ref[k : k + 1, a] * gcp[taps - k : taps - k + frames, a]
+            out = out * mask
+            g = jax.nn.sigmoid(pre_ref[:, b])
+            gpre[half, :, a_out] = (out * g).astype(jnp.bfloat16)
+            gpre[dp_n // 2 + half, :, a_out] = (
+                out * pre_ref[:, a] * g * (1.0 - g)
+            ).astype(jnp.bfloat16)
+
+        @pl.loop(0, part // 128)
+        def _(i):
+            start = half * part + i * 128
+            fn(i, pl.ds(pl.multiple_of(start, 128), 128),
+               pl.ds(pl.multiple_of(width + start, 128), 128),
+               pl.ds(pl.multiple_of(i * 128, 128), 128), None)
+
+    for half in range(dp_n // 2):
+        unconv(half)
+    for k, j in enumerate(line):
+        remote(gpre.at[j], cols_ref.at[d], as_.at[k], ar_.at[d], at(j, s)).start()
+    cols_ref[d] = gpre[d]
+
+    def tap_grads(a, b):
+        grad = gcp[body, a]
+        for k in range(taps):
+            kp_ref[k : k + 1, a] = jnp.sum(
+                grad * gp[k + 1 : k + 1 + frames, a], axis=0, keepdims=True
+            )
+        kp_ref[taps : taps + 1, a] = jnp.zeros((1, 128), jnp.float32)
+
+    blocks(tap_grads)
+    for k, j in enumerate(line):
+        copy = remote(gpre.at[j], cols_ref.at[j], as_.at[k], ar_.at[j], at(j, s))
         copy.wait_recv()
         copy.wait_send()
-    mid[...] = merge([near[j] for j in range(seq_n)], stats)
-    for k, j in enumerate(line):
-        remote(mid, far.at[d], s2.at[k], r2.at[d], at(j, s)).start()
-    far[d] = mid[...]
-    for k, j in enumerate(line):
-        copy = remote(mid, far.at[j], s2.at[k], r2.at[j], at(j, s))
-        copy.wait_recv()
-        copy.wait_send()
-    o_ref[...] = merge([far[j] for j in range(dp_n)], stats)
-
-
-def sum_all(vectors, stats, collective_id):
+
+
+def middle(pre_act, lengths, taps, gain, bias, up):
     dp_n, seq_n = lax.axis_size("dp"), lax.axis_size("seq")
-    blocks = vectors[0].shape[-1] // 128
-    stacked = jnp.stack([v.reshape(blocks, 128) for v in vectors])
-    stacked = jnp.pad(stacked, ((0, 0), (0, 16 - blocks), (0, 0)))
-    rows = 16 * len(vectors)
-    shape = (rows, 128)
-    out = pl.pallas_call(
-        functools.partial(sum_kernel, stats, dp_n, seq_n),
-        out_shape=jax.ShapeDtypeStruct(shape, jnp.float32),
-        in_specs=[VM],
-        out_specs=VM,
+    frames, width = up.shape
+    f32, bf, dma = jnp.float32, jnp.bfloat16, pltpu.SemaphoreType.DMA
+    pair = (2, width)
+    block = (dp_n, frames, 2 * width // dp_n)
+    return pl.pallas_call(
+        functools.partial(middle_kernel, dp_n, seq_n),
+        out_shape=(
+            jax.ShapeDtypeStruct(block, bf),
+            jax.ShapeDtypeStruct((taps.shape[0] + 1, width), f32),
+            jax.ShapeDtypeStruct((1, width), f32),
+            jax.ShapeDtypeStruct((1, width), f32),
+            jax.ShapeDtypeStruct(block, bf),
+        ),
+        in_specs=[VM, pl.BlockSpec(memory_space=pltpu.SMEM), VM, VM, VM, VM],
+        out_specs=(VM, VM, VM, VM, VM),
         scratch_shapes=[
-            pltpu.VMEM((seq_n,) + shape, jnp.float32),
-            pltpu.VMEM((dp_n,) + shape, jnp.float32),
-            pltpu.VMEM(shape, jnp.float32),
-            pltpu.SemaphoreType.DMA((seq_n,)),
-            pltpu.SemaphoreType.DMA((seq_n,)),
-            pltpu.SemaphoreType.DMA((dp_n,)),
-            pltpu.SemaphoreType.DMA((dp_n,)),
+            pltpu.VMEM((frames + 32, width), f32),
+            pltpu.VMEM((frames + 32, width), f32),
+            pltpu.VMEM((frames, width), f32),
+            pltpu.VMEM((frames, width), f32),
+            pltpu.VMEM((2, 16, width), bf),
+            pltpu.VMEM((2, 16, width), bf),
+            pltpu.VMEM((seq_n,) + pair, f32),
+            pltpu.VMEM((dp_n,) + pair, f32),
+            pltpu.VMEM(pair, f32),
+            pltpu.VMEM(pair, f32),
+            pltpu.VMEM((seq_n,) + pair, f32),
+            pltpu.VMEM((dp_n,) + pair, f32),
+            pltpu.VMEM(pair, f32),
+            pltpu.VMEM(pair, f32),
+            dma((2,)), dma((2,)), dma((2,)), dma((2,)),
+            dma((seq_n,)), dma((seq_n,)), dma((dp_n,)), dma((dp_n,)),
+            dma((seq_n,)), dma((seq_n,)), dma((dp_n,)), dma((dp_n,)),
+            dma((dp_n,)), dma((dp_n,)),
         ],
-        compiler_params=pltpu.CompilerParams(collective_id=collective_id, has_side_effects=True),
-    )(stacked.reshape(shape))
-    return out.reshape(len(vectors), 16, 128)[:, :blocks].reshape(len(vectors), blocks * 128)
+        compiler_params=pltpu.CompilerParams(collective_id=0, has_side_effects=True),
+    )(pre_act, lengths, taps, gain[None], bias[None], up)
 
 
 def square_at(s):
@@ -107,7 +258,7 @@
     return c, x, y, sx, sy, sd, sc
 
 
-def weights_kernel(w_ref, out, local, zs, zr, xs, xr, ys, yr, fs, fr, cs, cr):
+def weights_kernel(w_ref, codes_ref, scale_ref, out, x_all, x_ref, local, bs, br, zs, zr, xs, xr, ys, yr, fs, fr, cs, cr):
     d, s = lax.axis_index("dp"), lax.axis_index("seq")
     c, x, y, sx, sy, sd, sc = square_at(s)
     rows = w_ref.shape[1]
@@ -118,8 +269,17 @@
     greet([at(j, s) for j in line] + [px, py, pc])
     for k, j in enumerate(line):
         remote(w_ref.at[s], out.at[d, s], zs.at[k], zr.at[d], at(j, s)).start()
-    own = pltpu.make_async_copy(w_ref, out.at[d], local)
+    own = pltpu.make_async_copy(w_ref, out.at[d], local.at[0])
     own.start()
+    for i in range(scale_ref.shape[1]):
+        cols = slice(i * 128, i * 128 + 128)
+        x_ref[:, cols] = (
+            codes_ref[:, cols].astype(jnp.float32) * scale_ref[:, i : i + 1]
+        ).astype(jnp.bfloat16)
+    for k, j in enumerate(line):
+        remote(x_ref, x_all.at[d], bs.at[k], br.at[d], at(j, s)).start()
+    keep = pltpu.make_async_copy(x_ref, x_all.at[d], local.at[1])
+    keep.start()
     pending = []
     core = []
 
@@ -164,23 +324,33 @@
         copy.wait_send()
     for k, j in enumerate(line):
         remote(w_ref.at[s], out.at[d, s], zs.at[k], zr.at[d], at(j, s)).wait_send()
+    for k, j in enumerate(line):
+        copy = remote(x_ref, x_all.at[j], bs.at[k], br.at[j], at(j, s))
+        copy.wait_recv()
+        copy.wait_send()
     own.wait()
-
-
-def gather_weights(in_weight):
+    keep.wait()
+
+
+def gather_weights(in_weight, codes, scales):
     dp_n, seq_n = lax.axis_size("dp"), lax.axis_size("seq")
     rows, width = in_weight.shape
     dma = pltpu.SemaphoreType.DMA
-    out = pl.pallas_call(
+    hbm = pl.BlockSpec(memory_space=pl.ANY)
+    out, x_all, x = pl.pallas_call(
         weights_kernel,
-        out_shape=jax.ShapeDtypeStruct((dp_n, seq_n, rows // seq_n, width), in_weight.dtype),
-        in_specs=[VM],
-        out_specs=pl.BlockSpec(memory_space=pl.ANY),
-        scratch_shapes=[dma(()), dma((3,)), dma((4,)), dma((3,)), dma((3,)), dma((3,)), dma((3,)),
+        out_shape=(
+            jax.ShapeDtypeStruct((dp_n, seq_n, rows // seq_n, width), in_weight.dtype),
+            jax.ShapeDtypeStruct((dp_n,) + codes.shape, codes.dtype),
+            jax.ShapeDtypeStruct(codes.shape, codes.dtype),
+        ),
+        in_specs=[VM, VM, VM],
+        out_specs=(hbm, hbm, VM),
+        scratch_shapes=[dma((2,)), dma((3,)), dma((4,)), dma((3,)), dma((4,)), dma((3,)), dma((3,)), dma((3,)), dma((3,)),
                         dma((3, 2)), dma((3, 2)), dma((3, 5)), dma((3, 5))],
         compiler_params=pltpu.CompilerParams(collective_id=2, has_side_effects=True),
-    )(in_weight.reshape(seq_n, rows // seq_n, width))
-    return out.reshape(dp_n * rows, width)
+    )(in_weight.reshape(seq_n, rows // seq_n, width), codes, scales.T)
+    return out.reshape(dp_n * rows, width), x_all, x
 
 
 def grads_kernel(dp_n, seq_n, p_ref, kp_ref, o_ref, ko_ref, r0, acc, sa, sb, ra, rb, sa2, sb2, ra2,
@@ -211,7 +381,7 @@
         copy = remote(kp_ref.at[j], kb1.at[j], k1s.at[k], k1r.at[j], at(d, j))
         copy.wait_recv()
         copy.wait_send()
-    km[...] = merge([kb1[j] for j in range(seq_n)], False)
+    km[...] = total_of([kb1[j] for j in range(seq_n)])
     for k, j in enumerate(line):
         remote(km, kb2.at[d], k2s.at[k], k2r.at[d], at(j, s)).start()
     kb2[d] = km[...]
@@ -235,7 +405,7 @@
         copy = remote(km, kb2.at[j], k2s.at[k], k2r.at[j], at(j, s))
         copy.wait_recv()
         copy.wait_send()
-    ko_ref[s] = merge([kb2[j] for j in range(dp_n)], False)
+    ko_ref[s] = total_of([kb2[j] for j in range(dp_n)])
     for k, j in enumerate(plane):
         remote(ko_ref.at[s], ko_ref.at[s], k3s.at[k], k3r.at[s], at(d, j)).start()
     one.wait()
@@ -301,7 +471,7 @@
     dp_n, seq_n = lax.axis_size("dp"), lax.axis_size("seq")
     rows, width = partial.shape
     taps, channels = kernel_part.shape
-    packed = jnp.pad(kernel_part, ((0, 1), (0, 0))).reshape(seq_n, -1, 128)
+    packed = kernel_part.reshape(seq_n, -1, 128)
     block = packed.shape[1:]
     dma = pltpu.SemaphoreType.DMA
     bf = jnp.bfloat16
@@ -332,7 +502,7 @@
         ],
         compiler_params=pltpu.CompilerParams(collective_id=3, has_side_effects=True),
     )(partial, packed)
-    return summed.astype(jnp.float32), taps_sum.reshape(taps + 1, channels)[:taps]
+    return summed.astype(jnp.float32), taps_sum.reshape(taps, channels)[: taps - 1]
 
 
 def padded_2(cells, sides, width):
@@ -364,7 +534,7 @@
     return running
 
 
-def per_device(
+def plain(
     saved_codes, code_scales, lengths, in_weight, conv_kernel, bn_gain, bn_shift, out_grad
 ):
     frames = saved_codes.shape[1]
@@ -380,11 +550,7 @@
         :, None
     ]
     restored = restore(saved_codes[0], code_scales[0])
-    square = lax.axis_size("dp") == 4 and lax.axis_size("seq") == 8
-    if square:
-        weights = gather_weights(in_weight)
-    else:
-        weights = lax.all_gather(in_weight, "dp", axis=0, tiled=True)
+    weights = lax.all_gather(in_weight, "dp", axis=0, tiled=True)
     pre_act = lax.dot_general(
         restored, weights, (((1,), (1,)), ((), ())), preferred_element_type=jnp.float32
     )
@@ -393,15 +559,9 @@
     gated = (linear * gate_part * valid_mask).astype(jnp.bfloat16)
     gated_pad = padded_2(gated, (("seq", 0),), half_span)
     conv_out = depthwise(gated_pad, conv_kernel, frames)
-    own_sum = jnp.sum(conv_out * valid_mask, axis=0)
-    own_count = jnp.sum(valid_mask)
-    centered = (conv_out - own_sum / jnp.maximum(own_count, 1.0)) * valid_mask
-    own_square = jnp.sum(centered * centered, axis=0)
-    total, spread, _ = sum_all(
-        [own_sum, own_square, jnp.full_like(own_sum, own_count)], True, 0
-    )
-    mean_value = total / counted
-    variance = spread / counted
+    mean_value = lax.psum(jnp.sum(conv_out * valid_mask, axis=0), ("dp", "seq")) / counted
+    centered = (conv_out - mean_value) * valid_mask
+    variance = lax.psum(jnp.sum(centered * centered, axis=0), ("dp", "seq")) / counted
     inverse = lax.rsqrt(variance + EPS)
     normed = (conv_out - mean_value) * inverse
     shaped = bn_gain * normed + bn_shift
@@ -409,8 +569,8 @@
     grad_shaped = (
         out_grad[0].astype(jnp.float32) * valid_mask * smooth * (1.0 + shaped * (1.0 - smooth))
     )
-    shift_grad, gain_grad = sum_all(
-        [jnp.sum(grad_shaped, axis=0), jnp.sum(grad_shaped * normed, axis=0)], False, 1
+    shift_grad, gain_grad = lax.psum(
+        (jnp.sum(grad_shaped, axis=0), jnp.sum(grad_shaped * normed, axis=0)), ("dp", "seq")
     )
     grad_conv = (
         bn_gain * inverse * (grad_shaped - (shift_grad + normed * gain_grad) / counted) * valid_mask
@@ -421,6 +581,7 @@
             for offset in range(tap_count)
         ]
     )
+    kernel_grad = lax.psum(kernel_part, ("dp", "seq"))
     grad_pad = padded_2(grad_conv, (("seq", 0),), half_span)
     grad_gated = depthwise(grad_pad, conv_kernel[::-1], frames) * valid_mask
     grad_pre = jnp.concatenate(
@@ -434,12 +595,36 @@
         (((0, 1), (0, 1)), ((), ())),
         preferred_element_type=jnp.float32,
     )
-    if square:
-        weight_grad, kernel_grad = sum_grads(local_rows, kernel_part)
-    else:
-        weight_grad = lax.psum(local_rows, "seq")
-        kernel_grad = lax.psum(kernel_part, ("dp", "seq"))
+    weight_grad = lax.psum(local_rows, "seq")
     return (in_grad.astype(jnp.bfloat16)[None], weight_grad, kernel_grad, gain_grad, shift_grad)
+
+
+def per_device(
+    saved_codes, code_scales, lengths, in_weight, conv_kernel, bn_gain, bn_shift, out_grad
+):
+    if lax.axis_size("dp") != 4 or lax.axis_size("seq") != 8:
+        return plain(
+            saved_codes, code_scales, lengths, in_weight, conv_kernel, bn_gain, bn_shift, out_grad
+        )
+    weights, x_all, x = gather_weights(in_weight, saved_codes[0], code_scales[0])
+    pre_act = lax.dot_general(
+        x, weights, (((1,), (1,)), ((), ())), preferred_element_type=jnp.float32
+    )
+    own_columns, kernel_part, gain_grad, shift_grad, grad_pre = middle(
+        pre_act, lengths, conv_kernel, bn_gain, bn_shift, out_grad[0]
+    )
+    local_rows = lax.dot_general(
+        own_columns, x_all, (((0, 1), (0, 1)), ((), ())), preferred_element_type=jnp.float32
+    )
+    weight_grad, kernel_grad = sum_grads(local_rows, kernel_part)
+    part = weights.shape[0] // grad_pre.shape[0]
+    in_grad = lax.dot_general(
+        grad_pre, weights.reshape(-1, part, weights.shape[1]), (((0, 2), (0, 1)), ((), ())),
+        preferred_element_type=jnp.float32,
+    )
+    return (
+        in_grad.astype(jnp.bfloat16)[None], weight_grad, kernel_grad, gain_grad[0], shift_grad[0]
+    )
 
 
 def solution(mesh):

time: 247 us -> 194 us (0.79)
  other arithmetic: 45.3 us -> 5.73 us
  Pallas kernels: 127 us -> 163 us
  between operations: 17.2 us -> 0.7 us
  starting transfers between devices: 12.8 us -> 0 us
  waiting for transfers between devices: 11.5 us -> 0 us
  local copies, waits for them, and re-layouts: 15.3 us -> 6.36 us
    pallas_call x3 -> x2, Pallas kernels: 86.6 us -> 119 us  [the longest x1 68.4 us: gather_weights(): pl.pallas_call(weights_kernel, out_shape=(jax.ShapeDtypeStruct((dp_n, seq...]
    unnamed x1 -> x0, other arithmetic: 17 us -> none
    reduce_sum x9 -> x0, other arithmetic: 16.5 us -> none  [the longest x4 7.7 us: per_device(): jnp.sum(grad_conv * gated_pad[offset:offset + frames].astype(jnp.float32)...]
    all_to_all x1 -> x0, waiting for transfers between devices: 11.5 us -> none  [per_device(): lax.all_to_all(grad_pre[None], 'dp', split_axis=2, concat_axis=0, tiled=T...]
    ppermute x4 -> x0, starting transfers between devices: 8.96 us -> none  [the longest x2 6.25 us: padded_2(): lax.ppermute(tail, axis, [(i, (i + 1) % count) for i in range(ends)])]
    another operation x4 -> x0, other arithmetic: 4.82 us -> none
    another operation x33 -> x0, local copies, waits for them, and re-layouts: 4.79 us -> none  [the longest x32 4.07 us: per_device(): jnp.stack([jnp.sum(grad_conv * gated_pad[offset:offset + frames].astype(j...]
    pallas_call x1, Pallas kernels: 39.9 us -> 44.2 us  [sum_grads(): pl.pallas_call(functools.partial(grads_kernel, dp_n, seq_n), out_shape=(j...]
  transfers between devices with their start and end apart: 6 -> 0, of which waited for: 1 -> 0; matrix products, arithmetic and copies ran while one was open for 23% -> 0% of each run, Pallas kernels for 11% -> 0%
where the time goes in v2:
time: 194 us
  Pallas kernels  163 us (84%)
  matrix products  17.9 us (9%)
  local copies, waits for them, and re-layouts  6.36 us (3%)
  other arithmetic  5.73 us (3%)
    pallas_call x1, Pallas kernels, gather_weights(): pl.pallas_call(weights_kernel, out_shape=(jax.ShapeDtypeStruct((dp_n, seq...  68.4 us
    pallas_call x1, Pallas kernels, middle(): pl.pallas_call(functools.partial(middle_kernel, dp_n, seq_n), out_shape=(...  50.7 us
    pallas_call x1, Pallas kernels, sum_grads(): pl.pallas_call(functools.partial(grads_kernel, dp_n, seq_n), out_shape=(j...  44.2 us
    dot_general x1, matrix products, per_device(): lax.dot_general(x, weights, (((1,), (1,)), ((), ())), preferred_element_t...  8.05 us
    dot_general x1, matrix products, per_device(): lax.dot_general(grad_pre, weights.reshape(-1, part, weights.shape[1]), ((...  6.21 us
    convert_element_type x1, other arithmetic, sum_grads(): summed.astype(jnp.float32)  4.5 us

profile of v2, /device:TPU:0, one launch (start us, length us, event | category | flops | bytes accessed | tf_op | source)
XLA Modules:
  0.0 194.0 jit_solution(18238576687431138860)
XLA Ops:
  0.6 1.3 broadcast_in_dim.9.gain_ref
  1.9 1.3 broadcast_in_dim.10.bias_ref
  3.2 1.4 copy.13
  4.6 68.4 %shard_map.119 = (bf16[4,8,96,1536]{3,2,1,0:T(8,128)(2,1)}, bf16[4,128,1536]{2,1,0:T(8,128)(2,1)}, bf16[128,1536]{1,0:T(8,128)(2,1)}) custom-call(bf16[8,96,1536]{2,1,0:T(8,128)(2,1)} %bitcast.27, bf16[128,1536]{1,0:T(8,128)(2,1)} %bitcast.29, f32[128,12]{1,0:T(8,128)} %bitcast.30), custom_call_target="tpu_custom_call" | custom-call | tf_op jit(solution)/shard_map/pallas_call | solution.py:340
  73.0 8.0 %fusion.2.pre_ref = f32[128,3072]{1,0:T(8,128)} fusion(bf16[128,1536]{1,0:T(8,128)(2,1)} %get-tuple-element.15, bf16[3072,1536]{1,0:T(8,128)(2,1)} %bitcast.25), kind=kOutput, calls=%fused_computation.4 | convolution fusion | flops 1207959552 | bytes 11403264 | tf_op jit(solution)/shard_map/dot_general | solution.py:610
  81.1 50.7 %shard_map.120 = (bf16[4,128,768]{2,1,0:T(8,128)(2,1)}, f32[32,1536]{1,0:T(8,128)}, f32[1,1536]{1,0:T(1,128)}, f32[1,1536]{1,0:T(1,128)}, bf16[4,128,768]{2,1,0:T(8,128)(2,1)}) custom-call(f32[128,3072]{1,0:T(8,128)} %fusion.2.pre_ref, s32[4]{0:T(128)} %len_ref.1, f32[31,1536]{1,0:T(8,128)} %taps_ref.1, f32[1,1536]{1,0:T(1,128)} %broadcast_in_dim.9.gain_ref, ...), custom_call_target="tpu_custom_call" | custom-call | tf_op jit(solution)/shard_map/pallas_call | solution.py:217
  131.8 0.0 copy-start.4
  131.8 0.0 copy-start.3
  131.8 0.0 copy-start.2
  131.9 0.0 copy-start
  131.9 0.0 copy-start.1
  131.9 6.2 %fusion.1 = bf16[1,128,1536]{2,1,0:T(8,128)(2,1)} fusion(bf16[4,128,768]{2,1,0:T(8,128)(2,1)} %get-tuple-element.17, bf16[4,768,1536]{2,1,0:T(8,128)(2,1)} %bitcast.26), kind=kOutput, calls=%fused_computation.3 | convolution fusion | flops 1208156160 | bytes 10616832 | tf_op jit(solution)/shard_map/dot_general | solution.py:621
  138.1 0.0 copy-done.4
  138.1 0.6 reduce
  138.7 0.0 copy-done.3
  138.7 0.6 reduce.1
  139.3 0.0 copy-done.2
  139.3 0.7 reshape.24.kp_ref
  140.0 0.0 copy-done
  140.0 0.0 copy-done.1
  140.0 3.6 %convolution_bitcast_fusion.p_ref = f32[768,1536]{1,0:T(8,128)} fusion(bf16[4,128,768]{2,1,0:T(8,128)(2,1)S(1)} %copy-done.1, bf16[4,128,1536]{2,1,0:T(8,128)(2,1)S(1)} %copy-done), kind=kOutput, calls=%fused_computation | convolution fusion | flops 1207959552 | bytes 7077888 | tf_op jit(solution)/shard_map/dot_general | solution.py:616
  143.6 44.2 %shard_map.121 = (bf16[768,1536]{1,0:T(8,128)(2,1)}, f32[8,48,128]{2,1,0:T(8,128)}) custom-call(f32[768,1536]{1,0:T(8,128)} %convolution_bitcast_fusion.p_ref, f32[8,48,128]{2,1,0:T(8,128)} %reshape.24.kp_ref), custom_call_target="tpu_custom_call" | custom-call | tf_op jit(solution)/shard_map/pallas_call | solution.py:478
  187.9 1.6 reshape.25
  189.5 4.5 %convert_element_type.7 = f32[768,1536]{1,0:T(8,128)} convert(bf16[768,1536]{1,0:T(8,128)(2,1)} %get-tuple-element.21) | non-fusion elementwise | flops 1179648 | bytes 7077888 | tf_op jit(solution)/shard_map/convert_element_type | solution.py:505
Async XLA Ops:
  131.8 6.3 %copy-start.4 = (f32[1,1536]{1,0:T(1,128)S(1)}, f32[1,1536]{1,0:T(1,128)}, u32[]{:S(2)}) copy-start(f32[1,1536]{1,0:T(1,128)} %get-tuple-element.23) | copy-start | bytes 18436
  131.8 6.9 %copy-start.3 = (f32[1,1536]{1,0:T(1,128)S(1)}, f32[1,1536]{1,0:T(1,128)}, u32[]{:S(2)}) copy-start(f32[1,1536]{1,0:T(1,128)} %get-tuple-element.24) | copy-start | bytes 18436
  131.8 7.5 %copy-start.2 = (f32[32,1536]{1,0:T(8,128)S(1)}, f32[32,1536]{1,0:T(8,128)}, u32[]{:S(2)}) copy-start(f32[32,1536]{1,0:T(8,128)} %get-tuple-element.20) | copy-start | bytes 589828
  131.9 8.2 %copy-start = (bf16[4,128,1536]{2,1,0:T(8,128)(2,1)S(1)}, bf16[4,128,1536]{2,1,0:T(8,128)(2,1)}, u32[]{:S(2)}) copy-start(bf16[4,128,1536]{2,1,0:T(8,128)(2,1)} %get-tuple-element.19) | copy-start | bytes 4718596
  131.9 8.2 %copy-start.1 = (bf16[4,128,768]{2,1,0:T(8,128)(2,1)S(1)}, bf16[4,128,768]{2,1,0:T(8,128)(2,1)}, u32[]{:S(2)}) copy-start(bf16[4,128,768]{2,1,0:T(8,128)(2,1)} %get-tuple-element.18) | copy-start | bytes 2359300

commit v3 on v2

--- a/solution.py
+++ b/solution.py
@@ -48,7 +48,7 @@
     return total, spread
 
 
-def middle_kernel(dp_n, seq_n, pre_ref, len_ref, taps_ref, gain_ref, bias_ref, up_ref,
+def middle_kernel(dp_n, seq_n, pre_ref, len_ref, taps_ref, norm_ref, up_ref,
                   cols_ref, kp_ref, gg_ref, sg_ref, gpre,
                   gp, gcp, co, gs, hs, hr, near, far, st, mid, near2, far2, st2, mid2,
                   h_s, h_r, g_s, g_r, s1, r1, s2, r2, s3, r3, s4, r4, as_, ar_):
@@ -131,7 +131,7 @@
 
     def shape(a, b):
         normed = (co[:, a] - mid[0:1, a]) * mid[1:2, a]
-        shaped = gain_ref[:, a] * normed + bias_ref[:, a]
+        shaped = norm_ref[0:1, a] * normed + norm_ref[1:2, a]
         smooth = jax.nn.sigmoid(shaped)
         grad = up_ref[:, a].astype(jnp.float32) * mask * smooth * (1.0 + shaped * (1.0 - smooth))
         co[:, a] = normed
@@ -148,7 +148,7 @@
     gg_ref[...] = both[1:2]
 
     def back(a, b):
-        scale = gain_ref[:, a] * mid[1:2, a]
+        scale = norm_ref[0:1, a] * mid[1:2, a]
         gcp[body, a] = (
             scale * (gs[:, a] - (sg_ref[:, a] + co[:, a] * gg_ref[:, a]) / counted) * mask
         )
@@ -223,7 +223,7 @@
             jax.ShapeDtypeStruct((1, width), f32),
             jax.ShapeDtypeStruct(block, bf),
         ),
-        in_specs=[VM, pl.BlockSpec(memory_space=pltpu.SMEM), VM, VM, VM, VM],
+        in_specs=[VM, pl.BlockSpec(memory_space=pltpu.SMEM), VM, VM, VM],
         out_specs=(VM, VM, VM, VM, VM),
         scratch_shapes=[
             pltpu.VMEM((frames + 32, width), f32),
@@ -246,7 +246,7 @@
             dma((dp_n,)), dma((dp_n,)),
         ],
         compiler_params=pltpu.CompilerParams(collective_id=0, has_side_effects=True),
-    )(pre_act, lengths, taps, gain[None], bias[None], up)
+    )(pre_act, lengths, taps, jnp.stack([gain, bias]), up)
 
 
 def square_at(s):
@@ -258,17 +258,69 @@
     return c, x, y, sx, sy, sd, sc
 
 
-def weights_kernel(w_ref, codes_ref, scale_ref, out, x_all, x_ref, local, bs, br, zs, zr, xs, xr, ys, yr, fs, fr, cs, cr):
+def weights_kernel(w_ref, codes_ref, scale_ref, out, x_all, x_ref, local, bu, bd, br, zu, zd, zr,
+                   xs, xr, ys, yr, fs, fr, cs, cr):
     d, s = lax.axis_index("dp"), lax.axis_index("seq")
+    top = br.shape[0] - 1
     c, x, y, sx, sy, sd, sc = square_at(s)
-    rows = w_ref.shape[1]
-    half = rows // 2
+    half = w_ref.shape[1] // 2
     low, high = pl.ds(0, half), pl.ds(half, half)
     line = [d + 1 - 2 * lax.rem(d, 2), 2 - d // 2, 3 - 3 * (d // 2)]
     px, py, pc = at(d, sx), at(d, sy), at(d, sc)
     greet([at(j, s) for j in line] + [px, py, pc])
-    for k, j in enumerate(line):
-        remote(w_ref.at[s], out.at[d, s], zs.at[k], zr.at[d], at(j, s)).start()
+
+    def ends(src, dst, up, down, recv, act):
+        @pl.when(d < top)
+        def _():
+            act(remote(src, dst, up.at[d], recv.at[d], at(d + 1, s)))
+
+        @pl.when(d > 0)
+        def _():
+            act(remote(src, dst, down.at[d], recv.at[d], at(d - 1, s)))
+
+    def hop(h, ref, up, down, recv, arrive, act):
+        @pl.when(d - 1 - h >= 0)
+        def _():
+            j = d - 1 - h
+            if arrive is not None:
+                remote(ref(j), ref(j), up.at[j], recv.at[j], px).wait_recv()
+
+            @pl.when(d < top)
+            def _():
+                act(remote(ref(j), ref(j), up.at[j], recv.at[j], at(d + 1, s)))
+
+            if arrive is not None:
+                arrive(j)
+
+        @pl.when(d + 1 + h <= top)
+        def _():
+            j = d + 1 + h
+            if arrive is not None:
+                remote(ref(j), ref(j), down.at[j], recv.at[j], px).wait_recv()
+
+            @pl.when(d > 0)
+            def _():
+                act(remote(ref(j), ref(j), down.at[j], recv.at[j], at(d - 1, s)))
+
+            if arrive is not None:
+                arrive(j)
+
+    def start(copy):
+        copy.start()
+
+    def sent(copy):
+        copy.wait_send()
+
+    def nothing(j):
+        pass
+
+    def piece(j):
+        return out.at[j, s]
+
+    def frames_of(j):
+        return x_all.at[j]
+
+    ends(w_ref.at[s], out.at[d, s], zu, zd, zr, start)
     own = pltpu.make_async_copy(w_ref, out.at[d], local.at[0])
     own.start()
     for i in range(scale_ref.shape[1]):
@@ -276,58 +328,62 @@
         x_ref[:, cols] = (
             codes_ref[:, cols].astype(jnp.float32) * scale_ref[:, i : i + 1]
         ).astype(jnp.bfloat16)
-    for k, j in enumerate(line):
-        remote(x_ref, x_all.at[d], bs.at[k], br.at[d], at(j, s)).start()
     keep = pltpu.make_async_copy(x_ref, x_all.at[d], local.at[1])
     keep.start()
+    cx, cy, cd = sx + 1 - 2 * c, sy + 1 - 2 * c, sd + 1 - 2 * c
+
+    def spread(j):
+        mine = out.at[j, s]
+        return [
+            remote(mine, mine, xs.at[j], xr.at[j], px),
+            remote(mine, mine, ys.at[j], yr.at[j], py),
+            remote(mine, mine, cs.at[j, 0], cr.at[j, 0], pc),
+        ]
+
+    def arrive(j):
+        for copy in spread(j):
+            copy.start()
+
+    def own_copy(ref, send, recv, peer):
+        return remote(ref, ref, send, recv, peer)
+
+    for h in range(top):
+        hop(h, piece, zu, zd, zr, arrive, start)
+    ends(x_ref, x_all.at[d], bu, bd, br, start)
     pending = []
-    core = []
-
-    def to_core(k, n, ref, other):
-        copy = remote(ref, ref, cs.at[k, n], cr.at[k, n], pc)
+
+    def go(copy):
         copy.start()
         pending.append(copy)
-        core.append(remote(other, other, cs.at[k, n], cr.at[k, n], pc))
-
-    cx, cy, cd = sx + 1 - 2 * c, sy + 1 - 2 * c, sd + 1 - 2 * c
+
     for k, j in enumerate(line):
-        mine = out.at[j, s]
-        remote(mine, mine, zs.at[k], zr.at[j], at(j, s)).wait_recv()
-        for send, recv, peer in ((xs, xr, px), (ys, yr, py)):
-            copy = remote(mine, mine, send.at[k], recv.at[k], peer)
-            copy.start()
-            pending.append(copy)
-        to_core(k, 0, mine, out.at[j, sc])
-    for k, j in enumerate(line):
-        remote(out.at[j, sx], out.at[j, sx], xs.at[k], xr.at[k], px).wait_recv()
-        part = out.at[j, sx, low]
-        copy = remote(part, part, fs.at[k, 0], fr.at[k, 0], py)
-        copy.start()
-        pending.append(copy)
-        to_core(k, 1, out.at[j, sx], out.at[j, cx])
-        remote(out.at[j, sy], out.at[j, sy], ys.at[k], yr.at[k], py).wait_recv()
-        part = out.at[j, sy, high]
-        copy = remote(part, part, fs.at[k, 1], fr.at[k, 1], px)
-        copy.start()
-        pending.append(copy)
-        to_core(k, 2, out.at[j, sy], out.at[j, cy])
-    for k, j in enumerate(line):
+        own_copy(out.at[j, sx], xs.at[j], xr.at[j], px).wait_recv()
+        go(own_copy(out.at[j, sx, low], fs.at[j, 0], fr.at[j, 0], py))
+        go(own_copy(out.at[j, sx], cs.at[j, 1], cr.at[j, 1], pc))
+        own_copy(out.at[j, sy], ys.at[j], yr.at[j], py).wait_recv()
+        go(own_copy(out.at[j, sy, high], fs.at[j, 1], fr.at[j, 1], px))
+        go(own_copy(out.at[j, sy], cs.at[j, 2], cr.at[j, 2], pc))
+        hop(k, frames_of, bu, bd, br, nothing, start)
+    for j in line:
         part = out.at[j, sd, low]
-        remote(part, part, fs.at[k, 0], fr.at[k, 0], py).wait_recv()
-        to_core(k, 3, part, out.at[j, cd, low])
+        own_copy(part, fs.at[j, 0], fr.at[j, 0], py).wait_recv()
+        go(own_copy(part, cs.at[j, 3], cr.at[j, 3], pc))
         part = out.at[j, sd, high]
-        remote(part, part, fs.at[k, 1], fr.at[k, 1], px).wait_recv()
-        to_core(k, 4, part, out.at[j, cd, high])
-    for copy in core:
-        copy.wait_recv()
+        own_copy(part, fs.at[j, 1], fr.at[j, 1], px).wait_recv()
+        go(own_copy(part, cs.at[j, 4], cr.at[j, 4], pc))
+    for j in line:
+        for n, part in enumerate((out.at[j, sc], out.at[j, cx], out.at[j, cy],
+                                  out.at[j, cd, low], out.at[j, cd, high])):
+            own_copy(part, cs.at[j, n], cr.at[j, n], pc).wait_recv()
+        for copy in spread(j):
+            copy.wait_send()
     for copy in pending:
         copy.wait_send()
-    for k, j in enumerate(line):
-        remote(w_ref.at[s], out.at[d, s], zs.at[k], zr.at[d], at(j, s)).wait_send()
-    for k, j in enumerate(line):
-        copy = remote(x_ref, x_all.at[j], bs.at[k], br.at[j], at(j, s))
-        copy.wait_recv()
-        copy.wait_send()
+    ends(w_ref.at[s], out.at[d, s], zu, zd, zr, sent)
+    ends(x_ref, x_all.at[d], bu, bd, br, sent)
+    for h in range(top):
+        hop(h, piece, zu, zd, zr, None, sent)
+        hop(h, frames_of, bu, bd, br, None, sent)
     own.wait()
     keep.wait()
 
@@ -346,14 +402,14 @@
         ),
         in_specs=[VM, VM, VM],
         out_specs=(hbm, hbm, VM),
-        scratch_shapes=[dma((2,)), dma((3,)), dma((4,)), dma((3,)), dma((4,)), dma((3,)), dma((3,)), dma((3,)), dma((3,)),
-                        dma((3, 2)), dma((3, 2)), dma((3, 5)), dma((3, 5))],
+        scratch_shapes=[dma((2,))] + [dma((dp_n,))] * 10
+        + [dma((dp_n, 2)), dma((dp_n, 2)), dma((dp_n, 5)), dma((dp_n, 5))],
         compiler_params=pltpu.CompilerParams(collective_id=2, has_side_effects=True),
     )(in_weight.reshape(seq_n, rows // seq_n, width), codes, scales.T)
     return out.reshape(dp_n * rows, width), x_all, x
 
 
-def grads_kernel(dp_n, seq_n, p_ref, kp_ref, o_ref, ko_ref, r0, acc, sa, sb, ra, rb, sa2, sb2, ra2,
+def grads_kernel(dp_n, seq_n, p_ref, kp_ref, g_ref, w_hbm, o_ref, ko_ref, ig_ref, wv, ia, wl, r0, acc, sa, sb, ra, rb, sa2, sb2, ra2,
                  rb2, kb1, km, kb2, ws, wr, k1s, k1r, k2s, k2r, k3s, k3r):
     d, s = lax.axis_index("dp"), lax.axis_index("seq")
     c, x, y, sx, sy, sd, sc = square_at(s)
@@ -371,12 +427,22 @@
         def _(i):
             fn(pl.multiple_of(i * 16, 16))
 
+    load = pltpu.make_async_copy(w_hbm, wv, wl)
+    load.start()
     greet([at(d, j) for j in plane] + [at(j, s) for j in line])
     first = remote(p_ref.at[span((1 - c) * h, h)], r0, ws.at[0], wr.at[0], pc)
     first.start()
     for k, j in enumerate(plane):
         remote(kp_ref.at[j], kb1.at[s], k1s.at[k], k1r.at[s], at(d, j)).start()
     kb1[s] = kp_ref[s]
+    load.wait()
+
+    def product(j):
+        return jnp.dot(g_ref[j], wv[j], preferred_element_type=jnp.float32)
+
+    ia[...] = product(0)
+    for j in range(1, dp_n // 2):
+        ia[...] += product(j)
     for k, j in enumerate(plane):
         copy = remote(kp_ref.at[j], kb1.at[j], k1s.at[k], k1r.at[j], at(d, j))
         copy.wait_recv()
@@ -401,6 +467,9 @@
     two = remote(sb, rb, ws.at[2], wr.at[2], py)
     one.start()
     two.start()
+    for j in range(dp_n // 2, dp_n):
+        ia[...] += product(j)
+    ig_ref[...] = ia[...].astype(jnp.bfloat16)
     for k, j in enumerate(line):
         copy = remote(km, kb2.at[j], k2s.at[k], k2r.at[j], at(j, s))
         copy.wait_recv()
@@ -467,7 +536,7 @@
         remote(ko_ref.at[s], ko_ref.at[s], k3s.at[k], k3r.at[s], at(d, j)).wait_send()
 
 
-def sum_grads(partial, kernel_part):
+def sum_grads(partial, kernel_part, grad_pre, weights):
     dp_n, seq_n = lax.axis_size("dp"), lax.axis_size("seq")
     rows, width = partial.shape
     taps, channels = kernel_part.shape
@@ -475,15 +544,19 @@
     block = packed.shape[1:]
     dma = pltpu.SemaphoreType.DMA
     bf = jnp.bfloat16
-    summed, taps_sum = pl.pallas_call(
+    summed, taps_sum, in_grad = pl.pallas_call(
         functools.partial(grads_kernel, dp_n, seq_n),
         out_shape=(
             jax.ShapeDtypeStruct((rows, width), bf),
             jax.ShapeDtypeStruct(packed.shape, jnp.float32),
+            jax.ShapeDtypeStruct((grad_pre.shape[1], width), bf),
         ),
-        in_specs=[VM, VM],
-        out_specs=(VM, VM),
+        in_specs=[VM, VM, VM, pl.BlockSpec(memory_space=pl.ANY)],
+        out_specs=(VM, VM, VM),
         scratch_shapes=[
+            pltpu.VMEM(weights.shape, bf),
+            pltpu.VMEM((grad_pre.shape[1], width), jnp.float32),
+            dma(()),
             pltpu.VMEM((rows // 2, width), jnp.float32),
             pltpu.VMEM((rows // 2, width), jnp.float32),
             pltpu.VMEM((rows // 8, width), bf),
@@ -501,8 +574,8 @@
             dma((seq_n,)), dma((seq_n,)), dma((dp_n,)), dma((dp_n,)), dma((seq_n,)), dma((seq_n,)),
         ],
         compiler_params=pltpu.CompilerParams(collective_id=3, has_side_effects=True),
-    )(partial, packed)
-    return summed.astype(jnp.float32), taps_sum.reshape(taps, channels)[: taps - 1]
+    )(partial, packed, grad_pre, weights)
+    return summed.astype(jnp.float32), taps_sum.reshape(taps, channels)[: taps - 1], in_grad
 
 
 def padded_2(cells, sides, width):
@@ -616,14 +689,12 @@
     local_rows = lax.dot_general(
         own_columns, x_all, (((0, 1), (0, 1)), ((), ())), preferred_element_type=jnp.float32
     )
-    weight_grad, kernel_grad = sum_grads(local_rows, kernel_part)
     part = weights.shape[0] // grad_pre.shape[0]
-    in_grad = lax.dot_general(
-        grad_pre, weights.reshape(-1, part, weights.shape[1]), (((0, 2), (0, 1)), ((), ())),
-        preferred_element_type=jnp.float32,
+    weight_grad, kernel_grad, in_grad = sum_grads(
+        local_rows, kernel_part, grad_pre, weights.reshape(-1, part, weights.shape[1])
     )
     return (
-        in_grad.astype(jnp.bfloat16)[None], weight_grad, kernel_grad, gain_grad[0], shift_grad[0]
+        in_grad[None], weight_grad, kernel_grad, gain_grad[0], shift_grad[0]
     )
 
 

time: 194 us -> 177 us (0.912)
  Pallas kernels: 163 us -> 153 us
  matrix products: 17.9 us -> 12.8 us
  local copies, waits for them, and re-layouts: 6.36 us -> 3.62 us
    pallas_call x1, Pallas kernels: 68.4 us -> 58 us  [gather_weights(): pl.pallas_call(weights_kernel, out_shape=(jax.ShapeDtypeStruct((dp_n, seq...]
    dot_general x1 -> x0, matrix products: 6.21 us -> none  [per_device(): lax.dot_general(grad_pre, weights.reshape(-1, part, weights.shape[1]), ((...]
    broadcast_in_dim x2 -> x0, local copies, waits for them, and re-layouts: 2.59 us -> none  [the longest x1 1.3 us: middle(): gain[None]]
where the time goes in v3:
time: 177 us
  Pallas kernels  153 us (86%)
  matrix products  12.8 us (7%)
  other arithmetic  6.42 us (4%)
  local copies, waits for them, and re-layouts  3.62 us (2%)
    pallas_call x1, Pallas kernels, gather_weights(): pl.pallas_call(weights_kernel, out_shape=(jax.ShapeDtypeStruct((dp_n, seq...  58 us
    pallas_call x1, Pallas kernels, middle(): pl.pallas_call(functools.partial(middle_kernel, dp_n, seq_n), out_shape=(...  51.2 us
    pallas_call x1, Pallas kernels, sum_grads(): pl.pallas_call(functools.partial(grads_kernel, dp_n, seq_n), out_shape=(j...  44.1 us
    dot_general x1, matrix products, per_device(): lax.dot_general(x, weights, (((1,), (1,)), ((), ())), preferred_element_t...  8.06 us
    dot_general x1, matrix products, per_device(): lax.dot_general(own_columns, x_all, (((0, 1), (0, 1)), ((), ())), preferr...  4.77 us
    convert_element_type x1, other arithmetic, sum_grads(): summed.astype(jnp.float32)  4.57 us

profile of v3, /device:TPU:0, one launch (start us, length us, event | category | flops | bytes accessed | tf_op | source)
XLA Modules:
  0.0 177.0 jit_solution(17017867633724652252)
XLA Ops:
  0.6 1.4 copy.13
  2.1 58.0 %shard_map.119 = (bf16[4,8,96,1536]{3,2,1,0:T(8,128)(2,1)}, bf16[4,128,1536]{2,1,0:T(8,128)(2,1)}, bf16[128,1536]{1,0:T(8,128)(2,1)}) custom-call(bf16[8,96,1536]{2,1,0:T(8,128)(2,1)} %bitcast.18, bf16[128,1536]{1,0:T(8,128)(2,1)} %bitcast.21, f32[128,12]{1,0:T(8,128)} %bitcast.22), custom_call_target="tpu_custom_call" | custom-call | tf_op jit(solution)/shard_map/pallas_call | solution.py:396
  60.1 0.0 copy-start.4
  60.1 0.0 copy-start.5
  60.1 8.1 %fusion.pre_ref = f32[128,3072]{1,0:T(8,128)} fusion(bf16[128,1536]{1,0:T(8,128)(2,1)} %get-tuple-element.16, bf16[3072,1536]{1,0:T(8,128)(2,1)} %bitcast.16), kind=kOutput, calls=%fused_computation.2 | convolution fusion | flops 1207959552 | bytes 11403264 | tf_op jit(solution)/shard_map/dot_general | solution.py:683
  68.2 0.0 copy-done.4
  68.2 0.0 copy-start
  68.2 0.0 copy-done.5
  68.2 0.6 pad_maximum_fusion.norm_ref
  68.8 51.2 %shard_map.120 = (bf16[4,128,768]{2,1,0:T(8,128)(2,1)}, f32[32,1536]{1,0:T(8,128)}, f32[1,1536]{1,0:T(1,128)}, f32[1,1536]{1,0:T(1,128)}, bf16[4,128,768]{2,1,0:T(8,128)(2,1)}) custom-call(f32[128,3072]{1,0:T(8,128)} %fusion.pre_ref, s32[4]{0:T(128)} %len_ref.1, f32[31,1536]{1,0:T(8,128)} %taps_ref.1, f32[2,1536]{1,0:T(2,128)} %pad_maximum_fusion.norm_ref, ...), custom_call_target="tpu_custom_call" | custom-call | tf_op jit(solution)/shard_map/pallas_call | solution.py:217
  120.1 0.0 copy-done
  120.1 0.0 copy-start.2
  120.1 4.8 %convolution_bitcast_fusion.p_ref = f32[768,1536]{1,0:T(8,128)} fusion(bf16[4,128,768]{2,1,0:T(8,128)(2,1)} %get-tuple-element.18, bf16[4,128,1536]{2,1,0:T(8,128)(2,1)S(1)} %copy-done), kind=kOutput, calls=%fused_computation | convolution fusion | flops 1207959552 | bytes 7077888 | tf_op jit(solution)/shard_map/dot_general | solution.py:689
  124.9 0.0 copy-done.2
  124.9 0.7 reshape.24.kp_ref
  125.6 44.1 %shard_map.121 = (bf16[768,1536]{1,0:T(8,128)(2,1)}, f32[8,48,128]{2,1,0:T(8,128)}, bf16[128,1536]{1,0:T(8,128)(2,1)}) custom-call(f32[768,1536]{1,0:T(8,128)} %convolution_bitcast_fusion.p_ref, f32[8,48,128]{2,1,0:T(8,128)} %reshape.24.kp_ref, bf16[4,128,768]{2,1,0:T(8,128)(2,1)} %get-tuple-element.21.g_ref, bf16[4,768,1536]{2,1,0:T(8,128)(2,1)} %bitcast.17), custom_call_target="tpu_custom_call" | custom-call | tf_op jit(solution)/shard_map/pallas_call | solution.py:547
  169.7 0.0 copy-start.3
  169.7 0.0 copy-start.7
  169.7 0.0 copy-start.6
  169.7 0.0 copy-start.1
  169.7 4.6 %convert_element_type.3 = f32[768,1536]{1,0:T(8,128)} convert(bf16[768,1536]{1,0:T(8,128)(2,1)} %get-tuple-element.23) | non-fusion elementwise | flops 1179648 | bytes 7077888 | tf_op jit(solution)/shard_map/convert_element_type | solution.py:578
  174.3 0.0 copy-done.3
  174.3 0.7 reshape.25
  175.0 0.0 copy-done.7
  175.0 0.6 reduce
  175.6 0.0 copy-done.6
  175.6 0.6 reduce.1
  176.2 0.0 copy-done.1
  176.2 0.7 copy.17
  (2 shorter events, 0.0 us)
Async XLA Ops:
  60.1 8.1 %copy-start.4 = (f32[1536]{0:T(1024)S(1)}, f32[1536]{0:T(1024)}, u32[]{:S(2)}) copy-start(f32[1536]{0:T(1024)} %param.14) | copy-start | bytes 18436
  60.1 8.1 %copy-start.5 = (f32[1536]{0:T(1024)S(1)}, f32[1536]{0:T(1024)}, u32[]{:S(2)}) copy-start(f32[1536]{0:T(1024)} %param.13) | copy-start | bytes 18436
  68.2 51.9 %copy-start = (bf16[4,128,1536]{2,1,0:T(8,128)(2,1)S(1)}, bf16[4,128,1536]{2,1,0:T(8,128)(2,1)}, u32[]{:S(2)}) copy-start(bf16[4,128,1536]{2,1,0:T(8,128)(2,1)} %get-tuple-element.19) | copy-start | bytes 4718596
  120.1 4.8 %copy-start.2 = (f32[32,1536]{1,0:T(8,128)S(1)}, f32[32,1536]{1,0:T(8,128)}, u32[]{:S(2)}) copy-start(f32[32,1536]{1,0:T(8,128)} %get-tuple-element.20) | copy-start | bytes 589828
  169.7 4.6 %copy-start.3 = (f32[8,48,128]{2,1,0:T(8,128)S(1)}, f32[8,48,128]{2,1,0:T(8,128)}, u32[]{:S(2)}) copy-start(f32[8,48,128]{2,1,0:T(8,128)} %get-tuple-element.24) | copy-start | bytes 589828
  169.7 5.3 %copy-start.7 = (f32[1,1536]{1,0:T(1,128)S(1)}, f32[1,1536]{1,0:T(1,128)}, u32[]{:S(2)}) copy-start(f32[1,1536]{1,0:T(1,128)} %get-tuple-element.25) | copy-start | bytes 18436
  169.7 5.9 %copy-start.6 = (f32[1,1536]{1,0:T(1,128)S(1)}, f32[1,1536]{1,0:T(1,128)}, u32[]{:S(2)}) copy-start(f32[1,1536]{1,0:T(1,128)} %get-tuple-element.26) | copy-start | bytes 18436
  169.7 6.5 %copy-start.1 = (bf16[128,1536]{1,0:T(8,128)(2,1)S(1)}, bf16[128,1536]{1,0:T(8,128)(2,1)}, u32[]{:S(2)}) copy-start(bf16[128,1536]{1,0:T(8,128)(2,1)} %get-tuple-element.22) | copy-start | bytes 1179652
